TPU v7x, 128 devices: a whole 4x4x4 slice. The times are simulated.
128 devices in a mesh: scan: 8 (over z, core), tile: 16 (over x, y).
Axes of the slice: x: 4, y: 4, z: 4, core: 2. Of those that a mesh axis runs over, the one named last changes fastest.
Arguments:
- object_tiles: float32 [16, 2, 2, 512, 512], P('tile'), may hold values from -5 to 5
- probe_wave: float32 [2, 256, 256], replicated, may hold values from -5 to 5
- patterns: float32 [512, 256, 256], P(('scan', 'tile')), may hold values from 0 to 2
- tile_of: int32 [512], P(('scan', 'tile')), may hold values from 0 to 15, as said below
- offsets: int32 [512, 2], P(('scan', 'tile')), may hold values from 0 to 256
- owner_map: int32 [16], replicated, may hold values from 0 to 15, each once
Outputs:
- object_grad: float32 [16, 2, 2, 512, 512], P('tile', None, None, 'scan')
- probe_grad: float32 [2, 256, 256], replicated
Inputs may be any that keep to these rules, and one draw needn't show every extreme that they name: `tile_of`: positions are in groups of 64 consecutive ones (one group for each index of scan). The 4 positions of one device read 4 different tiles. In every group exactly two tiles are read by 8 positions each and every other tile by at most 4.
All inputs are finite; a program needn't handle non-finite values.
Results may differ from a plain program's by a relative error of at most 0.0003.
Values sent between devices are 32-bit elements; how exact they have to be, the bound alone decides.
A program may use at most 128 MiB of HBM per device.

v0:
```python
import math

import jax
import jax.numpy as jnp
from jax import lax
from jax.sharding import PartitionSpec as P

prop_phase = 0.75


def make_tables(side):
    counter = jnp.arange(side, dtype=jnp.int32)
    product = counter[:, None] * counter[None, :] % side
    angle = 2.0 * math.pi / side * product.astype(jnp.float32)
    norm_factor = 1.0 / math.sqrt(side)
    four_real = jnp.cos(angle) * norm_factor
    four_imag = -jnp.sin(angle) * norm_factor
    freq = jnp.where(counter < side // 2, counter, counter - side).astype(jnp.float32)
    phase = prop_phase * (freq[:, None] ** 2 + freq[None, :] ** 2) / side
    return (four_real, four_imag, jnp.cos(phase), -jnp.sin(phase))


def real_product(left, right):
    return jnp.dot(left, right, precision=lax.Precision.HIGHEST, preferred_element_type=jnp.float32)


def complex_product(left_re, left_im, right_re, right_im):
    return (
        real_product(left_re, right_re) - real_product(left_im, right_im),
        real_product(left_re, right_im) + real_product(left_im, right_re),
    )


def transform(field_re, field_im, four_real, four_imag):
    temp_re, temp_im = complex_product(four_real, four_imag, field_re, field_im)
    return complex_product(temp_re, temp_im, four_real, four_imag)


def position_loss(probe_wave, patch, pattern, weight, tables):
    four_real, four_imag, prop_real, prop_imag = tables
    probe_re, probe_im = (probe_wave[0], probe_wave[1])
    first_re, first_im = (patch[0, 0], patch[0, 1])
    second_re, second_im = (patch[1, 0], patch[1, 1])
    enter_re = probe_re * first_re - probe_im * first_im
    enter_im = probe_re * first_im + probe_im * first_re
    spec_re, spec_im = transform(enter_re, enter_im, four_real, four_imag)
    moved_re = spec_re * prop_real - spec_im * prop_imag
    moved_im = spec_re * prop_imag + spec_im * prop_real
    back_re, back_im = transform(moved_re, moved_im, four_real, -four_imag)
    exit_re = back_re * second_re - back_im * second_im
    exit_im = back_re * second_im + back_im * second_re
    far_re, far_im = transform(exit_re, exit_im, four_real, four_imag)
    resid = far_re * far_re + far_im * far_im - pattern
    return 0.5 * weight * jnp.sum(resid * resid)


def lookup(table, indices):
    choices_row = jnp.arange(table.shape[0], dtype=jnp.int32)
    return jnp.sum(jnp.where(indices[..., None] == choices_row, table, 0), axis=-1)


def accumulate(tile_side, grads, starts):
    zero = jnp.zeros((), jnp.int32)
    total = jnp.zeros((2, 2, tile_side, tile_side), jnp.float32)

    def add_one(slot_index, running):
        start = (zero, zero, starts[slot_index, 0], starts[slot_index, 1])
        current = lax.dynamic_slice(running, start, grads.shape[1:])
        return lax.dynamic_update_slice(running, current + grads[slot_index], start)

    return lax.fori_loop(0, grads.shape[0], add_one, total)


def per_device(object_tiles, probe_wave, patterns, tile_of, offsets, owner_map):
    tile_count = lax.axis_size("tile")
    my_index = lax.axis_index("tile")
    pos_dev = tile_of.shape[0]
    probe_side = probe_wave.shape[-1]
    own_tile = object_tiles[0]
    tile_side = own_tile.shape[-1]
    tables = make_tables(probe_side)
    batched = jax.vmap(jax.grad(position_loss, argnums=(0, 1)), in_axes=(None, 0, 0, 0, None))
    zero = jnp.zeros((), jnp.int32)
    listed_tiles, listed_offsets = (
        lax.all_gather(tile_of, "tile", axis=0, tiled=True),
        lax.all_gather(offsets, "tile", axis=0, tiled=True),
    )
    listed_owner = lookup(owner_map, listed_tiles).reshape(tile_count, pos_dev)
    mine = listed_owner == my_index
    present = jnp.any(mine, axis=1)
    source_offsets = jnp.sum(
        jnp.where(mine[..., None], listed_offsets.reshape(tile_count, pos_dev, 2), 0), axis=1
    )
    reader_owner = lookup(owner_map, tile_of)
    selector = (reader_owner[:, None] == jnp.arange(tile_count, dtype=jnp.int32)[None, :]).astype(
        jnp.float32
    )

    def extract(offset):
        return lax.dynamic_slice(
            own_tile, (zero, zero, offset[0], offset[1]), (2, 2, probe_side, probe_side)
        )

    outgoing = (
        jax.vmap(extract)(source_offsets) * present.astype(jnp.float32)[:, None, None, None, None]
    )
    incoming = lax.all_to_all(outgoing, "tile", split_axis=0, concat_axis=0, tiled=True)
    patches = jnp.take(incoming, reader_owner, axis=0)
    probe_terms, patch_grads = batched(
        probe_wave, patches, patterns, jnp.ones((pos_dev,), jnp.float32), tables
    )
    returned = jnp.einsum("kn,kabxy->nabxy", selector, patch_grads, precision=lax.Precision.HIGHEST)
    arrived = lax.all_to_all(returned, "tile", split_axis=0, concat_axis=0, tiled=True)
    tile_grad = accumulate(tile_side, arrived, source_offsets)
    probe_part = jnp.sum(probe_terms, axis=0)
    object_part = lax.psum_scatter(tile_grad[None], "scan", scatter_dimension=3, tiled=True)
    probe_total = lax.psum(probe_part, ("scan", "tile"))
    count = tile_count * lax.axis_size("scan") * pos_dev
    return (object_part, probe_total / jnp.sqrt(jnp.ones((), jnp.float32) * count))


def solution(mesh):
    return jax.shard_map(
        per_device,
        mesh=mesh,
        in_specs=(
            P("tile", None, None, None, None),
            P(),
            P(("scan", "tile"), None, None),
            P(("scan", "tile")),
            P(("scan", "tile"), None),
            P(),
        ),
        out_specs=(P("tile", None, None, "scan", None), P()),
        check_vma=False,
    )
```

profile of v0, /device:TPU:1, one launch (start us, length us, event | category | flops | bytes accessed | tf_op | source)
XLA Modules:
  0.0 1050.2 jit_solution(7578935066658738595)
XLA Ops:
  10.8 13.8 %all-reduce.6 = s32[64]{0:T(128)S(1)} all-reduce(s32[64]{0:T(128)S(1)} %dynamic-update-slice.2), channel_id=1, replica_groups=mesh['scan'=8,'tile'=16] {'tile'}, use_global_device_ids=true, to_apply=%add.6 | all-reduce | flops 64 | bytes 512
  25.4 16.1 %all-gather = s32[16,4,2]{1,2,0:T(2,128)S(1)} all-gather(s32[1,4,2]{1,2,0:T(2,128)} %bitcast.288), channel_id=1, replica_groups=mesh['scan'=8,'tile'=16] {'tile'}, dimensions={0}, use_global_device_ids=true | all-gather | bytes 544 | tf_op jit(solution)/shard_map/all_gather | solution.py:86
  42.2 76.8 %while.15 = (s32[]{:T(128)}, f32[2,2,512,512]{3,2,1,0:T(8,128)}, s32[16,4]{0,1:T(4,128)S(1)}, f32[16,2,2,256,256]{4,3,2,1,0:T(8,128)}, s32[]{:T(128)}) while((s32[]{:T(128)}, f32[2,2,512,512]{3,2,1,0:T(8,128)}, s32[16,4]{0,1:T(4,128)S(1)}, f32[16,2,2,256,256]{4,3,2,1,0:T(8,128)}, s32[]{:T(128)}) %tuple.76), condition=%wide.while_cond, body=%wide.while_body.sunk | while | flops 2 | bytes 2098801 | solution.py:100
  42.9 4.1 bitcast_dynamic-update-slice_fusion.2
  47.7 4.2 bitcast_dynamic-update-slice_fusion.2
  52.5 4.1 bitcast_dynamic-update-slice_fusion.2
  57.3 4.1 bitcast_dynamic-update-slice_fusion.2
  62.1 4.1 bitcast_dynamic-update-slice_fusion.2
  66.9 4.1 bitcast_dynamic-update-slice_fusion.2
  71.7 4.1 bitcast_dynamic-update-slice_fusion.2
  76.5 4.1 bitcast_dynamic-update-slice_fusion.2
  81.3 4.2 bitcast_dynamic-update-slice_fusion.2
  86.2 4.1 bitcast_dynamic-update-slice_fusion.2
  90.9 4.1 bitcast_dynamic-update-slice_fusion.2
  95.7 4.1 bitcast_dynamic-update-slice_fusion.2
  100.5 4.2 bitcast_dynamic-update-slice_fusion.2
  105.3 4.1 bitcast_dynamic-update-slice_fusion.2
  110.1 4.1 bitcast_dynamic-update-slice_fusion.2
  114.9 4.1 bitcast_dynamic-update-slice_fusion.2
  119.1 11.7 %broadcast_multiply_fusion = f32[16,2,2,256,256]{4,3,2,1,0:T(8,128)} fusion(f32[16,2,2,256,256]{4,3,2,1,0:T(8,128)} %get-tuple-element.89, f32[16]{0:T(128)S(1)} %convert_element_type.131), kind=kLoop, calls=%fused_computation.6 | loop fusion | flops 4194304 | bytes 33554496 | tf_op jit(solution)/shard_map/mul | solution.py:105
  130.8 5.3 all-to-all-start
  137.7 220.1 %all-to-all-done = f32[16,2,2,256,256]{4,3,2,1,0:T(8,128)} async-done(((f32[16,2,2,256,256]{4,3,2,1,0:T(8,128)}), f32[16,2,2,256,256]{4,3,2,1,0:T(8,128)}, u32[]{:S(2)}, u32[]{:S(2)}) %all-to-all-start) | async-done | bytes 16777248 | tf_op jit(solution)/shard_map/all_to_all | solution.py:107
  357.8 8.5 gather_fusion
  451.4 3.1 fusion.5
  462.9 3.0 convolution_add_fusion.3
  474.9 2.9 add_bitcast_fusion.1
  478.2 9.2 fusion
  487.4 19.2 %copy.127 = f32[16,2,2,256,256]{4,3,2,1,0:T(8,128)} copy(f32[16,2,2,256,256]{4,0,3,2,1:T(8,128)S(1)} %fusion) | data formatting | bytes 33554432 | tf_op jit(solution)/shard_map/kn,kabxy->nabxy/dot_general | solution.py:112
  506.6 8.6 all-to-all-start.1
  516.3 199.4 %all-to-all-done.1 = f32[16,2,2,256,256]{4,3,2,1,0:T(8,128)} async-done(((f32[16,2,2,256,256]{4,3,2,1,0:T(8,128)}), f32[16,2,2,256,256]{4,3,2,1,0:T(8,128)}, u32[]{:S(2)}, u32[]{:S(2)}) %all-to-all-start.1) | async-done | bytes 16777248 | tf_op jit(solution)/shard_map/all_to_all | solution.py:113
  718.2 275.5 %while.14 = (s32[]{:T(128)}, f32[2,2,512,512]{3,2,1,0:T(8,128)}, s32[16,2]{0,1:T(2,128)S(1)}, f32[16,2,2,256,256]{4,3,2,1,0:T(8,128)}, s32[]{:T(128)}, /*index=5*/s32[]{:T(128)}, s32[]{:T(128)}) while((s32[]{:T(128)}, f32[2,2,512,512]{3,2,1,0:T(8,128)}, s32[16,2]{0,1:T(2,128)S(1)}, f32[16,2,2,256,256]{4,3,2,1,0:T(8,128)}, s32[]{:T(128)}, ...), condition=%wide.region_5.6_spmd, body=%wide.region_4.5_spmd.sunk | while | flops 262152 | bytes 5243061 | solution.py:71
  724.5 10.8 %dynamic_update_slice.8 = f32[2,2,512,512]{3,2,1,0:T(8,128)} dynamic-update-slice(f32[2,2,512,512]{3,2,1,0:T(8,128)} %get-tuple-element.228, f32[2,2,256,256]{3,2,1,0:T(8,128)S(1)} %bitcast_add_fusion.2, s32[]{:T(128)} %constant.74.clone.1..sunk, s32[]{:T(128)} %constant.74.clone.1..sunk, s32[]{:T(128)S(6)} %select_n.378, s32[]{:T(128)S(6)} %select_n.379) | dynamic-update-slice | bytes 2097156 | tf_op jit(solution)/shard_map/while/body/eval_jaxpr/dynamic_update_slice | solution.py:69
  741.5 10.8 %dynamic_update_slice.8 = f32[2,2,512,512]{3,2,1,0:T(8,128)} dynamic-update-slice(f32[2,2,512,512]{3,2,1,0:T(8,128)} %get-tuple-element.228, f32[2,2,256,256]{3,2,1,0:T(8,128)S(1)} %bitcast_add_fusion.2, s32[]{:T(128)} %constant.74.clone.1..sunk, s32[]{:T(128)} %constant.74.clone.1..sunk, s32[]{:T(128)S(6)} %select_n.378, s32[]{:T(128)S(6)} %select_n.379) | dynamic-update-slice | bytes 2097156 | tf_op jit(solution)/shard_map/while/body/eval_jaxpr/dynamic_update_slice | solution.py:69
  758.6 10.8 %dynamic_update_slice.8 = f32[2,2,512,512]{3,2,1,0:T(8,128)} dynamic-update-slice(f32[2,2,512,512]{3,2,1,0:T(8,128)} %get-tuple-element.228, f32[2,2,256,256]{3,2,1,0:T(8,128)S(1)} %bitcast_add_fusion.2, s32[]{:T(128)} %constant.74.clone.1..sunk, s32[]{:T(128)} %constant.74.clone.1..sunk, s32[]{:T(128)S(6)} %select_n.378, s32[]{:T(128)S(6)} %select_n.379) | dynamic-update-slice | bytes 2097156 | tf_op jit(solution)/shard_map/while/body/eval_jaxpr/dynamic_update_slice | solution.py:69
  775.7 11.5 %dynamic_update_slice.8 = f32[2,2,512,512]{3,2,1,0:T(8,128)} dynamic-update-slice(f32[2,2,512,512]{3,2,1,0:T(8,128)} %get-tuple-element.228, f32[2,2,256,256]{3,2,1,0:T(8,128)S(1)} %bitcast_add_fusion.2, s32[]{:T(128)} %constant.74.clone.1..sunk, s32[]{:T(128)} %constant.74.clone.1..sunk, s32[]{:T(128)S(6)} %select_n.378, s32[]{:T(128)S(6)} %select_n.379) | dynamic-update-slice | bytes 2097156 | tf_op jit(solution)/shard_map/while/body/eval_jaxpr/dynamic_update_slice | solution.py:69
  793.5 10.8 %dynamic_update_slice.8 = f32[2,2,512,512]{3,2,1,0:T(8,128)} dynamic-update-slice(f32[2,2,512,512]{3,2,1,0:T(8,128)} %get-tuple-element.228, f32[2,2,256,256]{3,2,1,0:T(8,128)S(1)} %bitcast_add_fusion.2, s32[]{:T(128)} %constant.74.clone.1..sunk, s32[]{:T(128)} %constant.74.clone.1..sunk, s32[]{:T(128)S(6)} %select_n.378, s32[]{:T(128)S(6)} %select_n.379) | dynamic-update-slice | bytes 2097156 | tf_op jit(solution)/shard_map/while/body/eval_jaxpr/dynamic_update_slice | solution.py:69
  810.5 10.8 %dynamic_update_slice.8 = f32[2,2,512,512]{3,2,1,0:T(8,128)} dynamic-update-slice(f32[2,2,512,512]{3,2,1,0:T(8,128)} %get-tuple-element.228, f32[2,2,256,256]{3,2,1,0:T(8,128)S(1)} %bitcast_add_fusion.2, s32[]{:T(128)} %constant.74.clone.1..sunk, s32[]{:T(128)} %constant.74.clone.1..sunk, s32[]{:T(128)S(6)} %select_n.378, s32[]{:T(128)S(6)} %select_n.379) | dynamic-update-slice | bytes 2097156 | tf_op jit(solution)/shard_map/while/body/eval_jaxpr/dynamic_update_slice | solution.py:69
  827.6 10.8 %dynamic_update_slice.8 = f32[2,2,512,512]{3,2,1,0:T(8,128)} dynamic-update-slice(f32[2,2,512,512]{3,2,1,0:T(8,128)} %get-tuple-element.228, f32[2,2,256,256]{3,2,1,0:T(8,128)S(1)} %bitcast_add_fusion.2, s32[]{:T(128)} %constant.74.clone.1..sunk, s32[]{:T(128)} %constant.74.clone.1..sunk, s32[]{:T(128)S(6)} %select_n.378, s32[]{:T(128)S(6)} %select_n.379) | dynamic-update-slice | bytes 2097156 | tf_op jit(solution)/shard_map/while/body/eval_jaxpr/dynamic_update_slice | solution.py:69
  844.6 10.8 %dynamic_update_slice.8 = f32[2,2,512,512]{3,2,1,0:T(8,128)} dynamic-update-slice(f32[2,2,512,512]{3,2,1,0:T(8,128)} %get-tuple-element.228, f32[2,2,256,256]{3,2,1,0:T(8,128)S(1)} %bitcast_add_fusion.2, s32[]{:T(128)} %constant.74.clone.1..sunk, s32[]{:T(128)} %constant.74.clone.1..sunk, s32[]{:T(128)S(6)} %select_n.378, s32[]{:T(128)S(6)} %select_n.379) | dynamic-update-slice | bytes 2097156 | tf_op jit(solution)/shard_map/while/body/eval_jaxpr/dynamic_update_slice | solution.py:69
  861.7 10.8 %dynamic_update_slice.8 = f32[2,2,512,512]{3,2,1,0:T(8,128)} dynamic-update-slice(f32[2,2,512,512]{3,2,1,0:T(8,128)} %get-tuple-element.228, f32[2,2,256,256]{3,2,1,0:T(8,128)S(1)} %bitcast_add_fusion.2, s32[]{:T(128)} %constant.74.clone.1..sunk, s32[]{:T(128)} %constant.74.clone.1..sunk, s32[]{:T(128)S(6)} %select_n.378, s32[]{:T(128)S(6)} %select_n.379) | dynamic-update-slice | bytes 2097156 | tf_op jit(solution)/shard_map/while/body/eval_jaxpr/dynamic_update_slice | solution.py:69
  878.8 10.8 %dynamic_update_slice.8 = f32[2,2,512,512]{3,2,1,0:T(8,128)} dynamic-update-slice(f32[2,2,512,512]{3,2,1,0:T(8,128)} %get-tuple-element.228, f32[2,2,256,256]{3,2,1,0:T(8,128)S(1)} %bitcast_add_fusion.2, s32[]{:T(128)} %constant.74.clone.1..sunk, s32[]{:T(128)} %constant.74.clone.1..sunk, s32[]{:T(128)S(6)} %select_n.378, s32[]{:T(128)S(6)} %select_n.379) | dynamic-update-slice | bytes 2097156 | tf_op jit(solution)/shard_map/while/body/eval_jaxpr/dynamic_update_slice | solution.py:69
  895.8 11.8 %dynamic_update_slice.8 = f32[2,2,512,512]{3,2,1,0:T(8,128)} dynamic-update-slice(f32[2,2,512,512]{3,2,1,0:T(8,128)} %get-tuple-element.228, f32[2,2,256,256]{3,2,1,0:T(8,128)S(1)} %bitcast_add_fusion.2, s32[]{:T(128)} %constant.74.clone.1..sunk, s32[]{:T(128)} %constant.74.clone.1..sunk, s32[]{:T(128)S(6)} %select_n.378, s32[]{:T(128)S(6)} %select_n.379) | dynamic-update-slice | bytes 2097156 | tf_op jit(solution)/shard_map/while/body/eval_jaxpr/dynamic_update_slice | solution.py:69
  913.9 11.6 %dynamic_update_slice.8 = f32[2,2,512,512]{3,2,1,0:T(8,128)} dynamic-update-slice(f32[2,2,512,512]{3,2,1,0:T(8,128)} %get-tuple-element.228, f32[2,2,256,256]{3,2,1,0:T(8,128)S(1)} %bitcast_add_fusion.2, s32[]{:T(128)} %constant.74.clone.1..sunk, s32[]{:T(128)} %constant.74.clone.1..sunk, s32[]{:T(128)S(6)} %select_n.378, s32[]{:T(128)S(6)} %select_n.379) | dynamic-update-slice | bytes 2097156 | tf_op jit(solution)/shard_map/while/body/eval_jaxpr/dynamic_update_slice | solution.py:69
  931.7 10.8 %dynamic_update_slice.8 = f32[2,2,512,512]{3,2,1,0:T(8,128)} dynamic-update-slice(f32[2,2,512,512]{3,2,1,0:T(8,128)} %get-tuple-element.228, f32[2,2,256,256]{3,2,1,0:T(8,128)S(1)} %bitcast_add_fusion.2, s32[]{:T(128)} %constant.74.clone.1..sunk, s32[]{:T(128)} %constant.74.clone.1..sunk, s32[]{:T(128)S(6)} %select_n.378, s32[]{:T(128)S(6)} %select_n.379) | dynamic-update-slice | bytes 2097156 | tf_op jit(solution)/shard_map/while/body/eval_jaxpr/dynamic_update_slice | solution.py:69
  948.8 10.8 %dynamic_update_slice.8 = f32[2,2,512,512]{3,2,1,0:T(8,128)} dynamic-update-slice(f32[2,2,512,512]{3,2,1,0:T(8,128)} %get-tuple-element.228, f32[2,2,256,256]{3,2,1,0:T(8,128)S(1)} %bitcast_add_fusion.2, s32[]{:T(128)} %constant.74.clone.1..sunk, s32[]{:T(128)} %constant.74.clone.1..sunk, s32[]{:T(128)S(6)} %select_n.378, s32[]{:T(128)S(6)} %select_n.379) | dynamic-update-slice | bytes 2097156 | tf_op jit(solution)/shard_map/while/body/eval_jaxpr/dynamic_update_slice | solution.py:69
  965.9 10.8 %dynamic_update_slice.8 = f32[2,2,512,512]{3,2,1,0:T(8,128)} dynamic-update-slice(f32[2,2,512,512]{3,2,1,0:T(8,128)} %get-tuple-element.228, f32[2,2,256,256]{3,2,1,0:T(8,128)S(1)} %bitcast_add_fusion.2, s32[]{:T(128)} %constant.74.clone.1..sunk, s32[]{:T(128)} %constant.74.clone.1..sunk, s32[]{:T(128)S(6)} %select_n.378, s32[]{:T(128)S(6)} %select_n.379) | dynamic-update-slice | bytes 2097156 | tf_op jit(solution)/shard_map/while/body/eval_jaxpr/dynamic_update_slice | solution.py:69
  982.9 10.8 %dynamic_update_slice.8 = f32[2,2,512,512]{3,2,1,0:T(8,128)} dynamic-update-slice(f32[2,2,512,512]{3,2,1,0:T(8,128)} %get-tuple-element.228, f32[2,2,256,256]{3,2,1,0:T(8,128)S(1)} %bitcast_add_fusion.2, s32[]{:T(128)} %constant.74.clone.1..sunk, s32[]{:T(128)} %constant.74.clone.1..sunk, s32[]{:T(128)S(6)} %select_n.378, s32[]{:T(128)S(6)} %select_n.379) | dynamic-update-slice | bytes 2097156 | tf_op jit(solution)/shard_map/while/body/eval_jaxpr/dynamic_update_slice | solution.py:69
  995.7 46.8 %reduce-scatter.2.cloned.1.call-done = f32[1,2,2,64,512]{4,3,2,1,0:T(8,128)} async-done(((f32[1,2,2,512,512]{4,3,2,1,0:T(8,128)}), f32[1,2,2,64,512]{4,3,2,1,0:T(8,128)}) %reduce-scatter.2.cloned.1.call-update) | async-done | bytes 524304 | tf_op jit(solution)/shard_map/reduce_scatter | solution.py:116
  (153 shorter events, 167.2 us)
Async XLA Ops:
  130.8 6.6 copy-start.2
  130.8 6.6 copy-start.3
  130.8 6.8 copy-start.1
  130.8 227.0 %all-to-all-start = ((f32[16,2,2,256,256]{4,3,2,1,0:T(8,128)}), f32[16,2,2,256,256]{4,3,2,1,0:T(8,128)}, u32[]{:S(2)}, u32[]{:S(2)}) async-start(f32[16,2,2,256,256]{4,3,2,1,0:T(8,128)} %broadcast_multiply_fusion), calls=%async_computation | async-start | bytes 33554432 | tf_op jit(solution)/shard_map/all_to_all | solution.py:107
  413.4 6.5 copy-start
  506.6 209.1 %all-to-all-start.1 = ((f32[16,2,2,256,256]{4,3,2,1,0:T(8,128)}), f32[16,2,2,256,256]{4,3,2,1,0:T(8,128)}, u32[]{:S(2)}, u32[]{:S(2)}) async-start(f32[16,2,2,256,256]{4,3,2,1,0:T(8,128)} %copy.127), calls=%async_computation.1 | async-start | bytes 33554432 | tf_op jit(solution)/shard_map/all_to_all | solution.py:113
  515.2 478.6 %all-reduce.9.cloned.1.call-start = ((), (), s32[]{:S(2)}) async-start(), calls=%async_computation.4 | async-start | bytes 1048576 | tf_op jit(solution)/shard_map/psum | solution.py:117
  516.3 526.1 %reduce-scatter.2.cloned.1.call-start = ((), (), s32[]{:S(2)}) async-start(), calls=%async_computation.3 | async-start | bytes 4718592 | tf_op jit(solution)/shard_map/reduce_scatter | solution.py:116
Sparse Core Ops, SparseCore 0:
  521.3 320.2 all-reduce.8
Sparse Core Ops, SparseCore 1:
  993.8 48.5 reduce-scatter.1
where the time goes:
time: 1070 us; the launch traced here: 1050 us
  waiting for transfers between devices  466 us (44%)
  local copies, waits for them, and re-layouts  295 us (28%)
  matrix products  117 us (11%)
  loops' own time  56.8 us (5%)
  other arithmetic  54.3 us (5%)
  blocking collectives  29.9 us (3%)
  between operations  17.1 us (2%)
  starting transfers between devices  14 us (1%)
    all_to_all x1, waiting for transfers between devices, per_device(): lax.all_to_all(outgoing, 'tile', split_axis=0, concat_axis=0, tiled=True)  220 us
    all_to_all x1, waiting for transfers between devices, per_device(): lax.all_to_all(returned, 'tile', split_axis=0, concat_axis=0, tiled=True)  199 us
    dynamic_update_slice x16, local copies, waits for them, and re-layouts, add_one(): return lax.dynamic_update_slice(running, current + grads[slot_index], start)  175 us
    dot_general x48, matrix products, real_product(): jnp.dot(left, right, precision=lax.Precision.HIGHEST, preferred_element_t...  108 us
    gather x48, local copies, waits for them, and re-layouts  76.7 us
    another operation x1, loops' own time, accumulate(): return lax.fori_loop(0, grads.shape[0], add_one, total)  56.8 us
    reduce_scatter x1, waiting for transfers between devices, per_device(): lax.psum_scatter(tile_grad[None], 'scan', scatter_dimension=3, tiled=True)  46.8 us
    add x16, other arithmetic, add_one(): return lax.dynamic_update_slice(running, current + grads[slot_index], start)  34 us
  transfers between devices with their start and end apart: 4, of which 3 were waited for; matrix products, arithmetic and copies ran while one was open for 21% of the time, Pallas kernels for 0%

commit v1 on v0

v1 whole, which is shorter than its diff:
```python
import functools
import math

import jax
import jax.numpy as jnp
import ml_dtypes
import numpy as np
from jax import lax
from jax.experimental import pallas as pl
from jax.experimental.pallas import tpu as pltpu
from jax.sharding import PartitionSpec as P

PROP_PHASE = 0.75
SIDE = 256
HALF = 128
MAX_READS = 8
F32 = jnp.float32
BF16 = jnp.bfloat16


def embed(block):
    return np.block([[block.real, block.imag], [-block.imag, block.real]])


@functools.cache
def tables():
    index = np.arange(SIDE)
    freq = np.where(index < HALF, index, index - SIDE).astype(np.float64)
    wave = np.exp(-2j * math.pi * (index[:, None] * index[None, :] % SIDE) / SIDE) / math.sqrt(SIDE)
    step = np.exp(-1j * PROP_PHASE * freq**2 / SIDE)
    travel = wave.conj() @ (step[:, None] * wave)
    plus = (travel[:HALF, :HALF] + travel[:HALF, HALF:]) / 2
    minus = (travel[:HALF, :HALF] - travel[:HALF, HALF:]) / 2
    forms = []
    for block in (plus, minus, wave[:HALF, 0::2], wave[:HALF, 1::2]):
        form = embed(block)
        forms += [form, form.T]
    forms = np.stack(forms)
    high = forms.astype(ml_dtypes.bfloat16)
    low = (forms - high.astype(np.float64)).astype(ml_dtypes.bfloat16)
    shuffle = np.zeros((SIDE, SIDE), ml_dtypes.bfloat16)
    shuffle[2 * np.arange(HALF), np.arange(HALF)] = 1
    shuffle[2 * np.arange(HALF) + 1, HALF + np.arange(HALF)] = 1
    return high, low, shuffle


A_PLUS, A_MINUS, F_EVEN, F_ODD = 0, 2, 4, 6


def parts(x):
    high = x.astype(BF16)
    return high, (x - high.astype(F32)).astype(BF16)


def mm(x, y):
    return jnp.dot(x, y, preferred_element_type=F32)


def right(x, high_ref, low_ref, which):
    xh, xl = parts(x)
    wh, wl = high_ref[which], low_ref[which]
    total = mm(xh, wh)
    total = total + mm(xl, wh)
    return total + mm(xh, wl)


def left(x, high_ref, low_ref, which):
    xh, xl = parts(x)
    wh, wl = high_ref[which], low_ref[which]
    total = mm(wh, xh)
    total = total + mm(wl, xh)
    return total + mm(wh, xl)


def cols(re, im):
    return (
        jnp.concatenate([re[:, :HALF] + re[:, HALF:], im[:, :HALF] + im[:, HALF:]], axis=1),
        jnp.concatenate([re[:, :HALF] - re[:, HALF:], im[:, :HALF] - im[:, HALF:]], axis=1),
    )


def rows(re, im):
    return (
        jnp.concatenate([re[:HALF] + re[HALF:], im[:HALF] + im[HALF:]], axis=0),
        jnp.concatenate([re[:HALF] - re[HALF:], im[:HALF] - im[HALF:]], axis=0),
    )


def split_cols(p, q):
    return (
        jnp.concatenate([p[:, :HALF], q[:, :HALF]], axis=1),
        jnp.concatenate([p[:, HALF:], q[:, HALF:]], axis=1),
    )


def split_rows(p, q):
    return (
        jnp.concatenate([p[:HALF], q[:HALF]], axis=0),
        jnp.concatenate([p[HALF:], q[HALF:]], axis=0),
    )


def travel(re, im, hi, lo, conj):
    flip = 1 if conj else 0
    s, d = cols(re, im)
    p, q = right(s, hi, lo, A_PLUS + flip), right(d, hi, lo, A_MINUS + flip)
    re, im = split_cols(p + q, p - q)
    s, d = rows(re, im)
    p, q = left(s, hi, lo, A_PLUS + 1 - flip), left(d, hi, lo, A_MINUS + 1 - flip)
    return split_rows(p + q, p - q)


def to_far(re, im, hi, lo):
    s, d = cols(re, im)
    re, im = split_cols(right(s, hi, lo, F_EVEN), right(d, hi, lo, F_ODD))
    s, d = rows(re, im)
    return split_rows(left(s, hi, lo, F_EVEN + 1), left(d, hi, lo, F_ODD + 1))


def from_far(re, im, hi, lo):
    even, odd = (
        jnp.concatenate([re[:, :HALF], im[:, :HALF]], axis=1),
        jnp.concatenate([re[:, HALF:], im[:, HALF:]], axis=1),
    )
    p, q = right(even, hi, lo, F_EVEN + 1), right(odd, hi, lo, F_ODD + 1)
    re, im = split_cols(p + q, p - q)
    even, odd = (
        jnp.concatenate([re[:HALF], im[:HALF]], axis=0),
        jnp.concatenate([re[HALF:], im[HALF:]], axis=0),
    )
    p, q = left(even, hi, lo, F_EVEN), left(odd, hi, lo, F_ODD)
    return split_rows(p + q, p - q)


def lane_mask(shift):
    return lax.broadcasted_iota(jnp.int32, (SIDE, HALF), 1) < shift


def spots(a, b):
    base = b // HALF
    return [pl.ds(4 * a + jnp.minimum(base + k, 3), SIDE, stride=4) for k in range(3)]


def patch(plane, a, b):
    shift = b % HALF
    back = lax.rem(HALF - shift, HALF)
    tiles = [pltpu.roll(plane[spot, :], back, 1) for spot in spots(a, b)]
    mask = lane_mask(HALF - shift)
    return jnp.concatenate(
        [jnp.where(mask, tiles[0], tiles[1]), jnp.where(mask, tiles[1], tiles[2])], axis=1
    )


def add_patch(plane, a, b, value):
    shift = b % HALF
    first, second = pltpu.roll(value[:, :HALF], shift, 1), pltpu.roll(value[:, HALF:], shift, 1)
    mask = lane_mask(shift)
    zero = jnp.zeros_like(first)
    terms = [jnp.where(mask, zero, first), jnp.where(mask, first, second), jnp.where(mask, second, zero)]
    for spot, term in zip(spots(a, b), terms):
        plane[spot, :] = plane[spot, :] + term


def open_tile(tile, held):
    for plane in range(4):
        for k in range(4):
            held[plane, pl.ds(k, 2 * SIDE, stride=4), :] = tile[
                plane // 2, plane % 2, :, k * HALF : (k + 1) * HALF
            ]


def close_tile(held, grad):
    for plane in range(4):
        for k in range(4):
            grad[0, plane // 2, plane % 2, :, k * HALF : (k + 1) * HALF] = held[
                plane, pl.ds(k, 2 * SIDE, stride=4), :
            ]


def forward_kernel(info, tile, probe, hi, lo, back, far, held):
    k = pl.program_id(0)

    @pl.when(k == 0)
    def _():
        open_tile(tile, held)

    @pl.when(k < info[3 * MAX_READS])
    def _():
        a, b = info[MAX_READS + k], info[2 * MAX_READS + k]
        ore, oim = patch(held.at[0], a, b), patch(held.at[1], a, b)
        pre, pim = probe[0], probe[1]
        re, im = travel(pre * ore - pim * oim, pre * oim + pim * ore, hi, lo, False)
        back[0, 0], back[0, 1] = re, im
        ore, oim = patch(held.at[2], a, b), patch(held.at[3], a, b)
        far[0, 0], far[0, 1] = to_far(re * ore - im * oim, re * oim + im * ore, hi, lo)


def backward_kernel(
    info, tile, probe, hi, lo, shuffle, back, far, pattern, grad, probe_grad, held, total, mixed
):
    k = pl.program_id(0)

    @pl.when(k == 0)
    def _():
        open_tile(tile, held)
        total[...] = jnp.zeros_like(total)
        probe_grad[...] = jnp.zeros_like(probe_grad)

    @pl.when(k < info[3 * MAX_READS])
    def _():
        a, b = info[MAX_READS + k], info[2 * MAX_READS + k]
        for c in range(2):
            mixed[c] = pattern[0, :, c * HALF : (c + 1) * HALF]
        measured = jnp.concatenate(
            [
                jnp.concatenate([mixed[c, pl.ds(odd, HALF, stride=2), :] for c in range(2)], axis=1)
                for odd in range(2)
            ],
            axis=0,
        )
        mh, ml = parts(measured)
        measured = mm(mh, shuffle[...]) + mm(ml, shuffle[...])
        fre, fim = far[0, 0], far[0, 1]
        scale = 2.0 * (fre * fre + fim * fim - measured)
        gre, gim = from_far(scale * fre, scale * fim, hi, lo)
        bre, bim = back[0, 0], back[0, 1]
        add_patch(total.at[2], a, b, bre * gre + bim * gim)
        add_patch(total.at[3], a, b, bre * gim - bim * gre)
        ore, oim = patch(held.at[2], a, b), patch(held.at[3], a, b)
        gre, gim = travel(ore * gre + oim * gim, ore * gim - oim * gre, hi, lo, True)
        pre, pim = probe[0], probe[1]
        add_patch(total.at[0], a, b, pre * gre + pim * gim)
        add_patch(total.at[1], a, b, pre * gim - pim * gre)
        ore, oim = patch(held.at[0], a, b), patch(held.at[1], a, b)
        probe_grad[0] += ore * gre + oim * gim
        probe_grad[1] += ore * gim - oim * gre

    @pl.when(k == pl.num_programs(0) - 1)
    def _():
        close_tile(total, grad)


def plane_scratch():
    return pltpu.VMEM((4, 2 * SIDE * 4, HALF), F32)


def whole(array):
    ndim = array.ndim
    return pl.BlockSpec(array.shape, lambda k, info: (0,) * ndim, pipeline_mode=pl.Buffered(1))


def forward(info, tile, probe, hi, lo):
    block = pl.BlockSpec((1, 2, SIDE, SIDE), lambda k, info: (k, 0, 0, 0))
    out = jax.ShapeDtypeStruct((MAX_READS, 2, SIDE, SIDE), F32)
    return pl.pallas_call(
        forward_kernel,
        out_shape=(out, out),
        grid_spec=pltpu.PrefetchScalarGridSpec(
            num_scalar_prefetch=1,
            grid=(MAX_READS,),
            in_specs=[whole(x) for x in (tile, probe, hi, lo)],
            out_specs=(block, block),
            scratch_shapes=[plane_scratch()],
        ),
        cost_estimate=pl.CostEstimate(
            flops=MAX_READS * 24 * 2 * SIDE**3, bytes_accessed=14 << 20, transcendentals=0
        ),
        compiler_params=pltpu.CompilerParams(vmem_limit_bytes=48 << 20),
    )(info, tile, probe, hi, lo)


def backward(info, tile, probe, hi, lo, shuffle, back, far, arrived):
    block = pl.BlockSpec((1, 2, SIDE, SIDE), lambda k, info: (k, 0, 0, 0))
    pattern = pl.BlockSpec((1, SIDE, SIDE), lambda k, info: (info[k], 0, 0))
    grad = jax.ShapeDtypeStruct((1,) + tile.shape, F32)
    probe_grad = jax.ShapeDtypeStruct(probe.shape, F32)
    return pl.pallas_call(
        backward_kernel,
        out_shape=(grad, probe_grad),
        grid_spec=pltpu.PrefetchScalarGridSpec(
            num_scalar_prefetch=1,
            grid=(MAX_READS,),
            in_specs=[whole(x) for x in (tile, probe, hi, lo, shuffle)] + [block, block, pattern],
            out_specs=(whole(grad), whole(probe_grad)),
            scratch_shapes=[plane_scratch(), plane_scratch(), pltpu.VMEM((2, SIDE, HALF), F32)],
        ),
        cost_estimate=pl.CostEstimate(
            flops=MAX_READS * 26 * 2 * SIDE**3, bytes_accessed=20 << 20, transcendentals=0
        ),
        compiler_params=pltpu.CompilerParams(vmem_limit_bytes=48 << 20),
    )(info, tile, probe, hi, lo, shuffle, back, far, arrived)


def spread_kernel(which, patterns, out, held, in_sem, out_sem):
    count = out.shape[0]
    load = pltpu.make_async_copy(patterns, held, in_sem)
    load.start()
    load.wait()
    copies = [pltpu.make_async_copy(held.at[which[j]], out.at[j], out_sem.at[j]) for j in range(count)]
    for copy in copies:
        copy.start()
    for copy in copies:
        copy.wait()


def spread(which, patterns):
    count = which.shape[0]
    return pl.pallas_call(
        spread_kernel,
        out_shape=jax.ShapeDtypeStruct((count,) + patterns.shape[1:], F32),
        in_specs=[pl.BlockSpec(memory_space=pltpu.SMEM), pl.BlockSpec(memory_space=pl.ANY)],
        out_specs=pl.BlockSpec(memory_space=pl.ANY),
        scratch_shapes=[
            pltpu.VMEM(patterns.shape, F32),
            pltpu.SemaphoreType.DMA,
            pltpu.SemaphoreType.DMA((count,)),
        ],
    )(which, patterns)


def lookup(table, indices):
    choices = jnp.arange(table.shape[0], dtype=jnp.int32)
    return jnp.sum(jnp.where(indices[..., None] == choices, table, 0), axis=-1)


def per_device(object_tiles, probe_wave, patterns, tile_of, offsets, owner_map):
    tile_count = lax.axis_size("tile")
    pos_dev = tile_of.shape[0]
    high, low, shuffle = tables()
    high, low, shuffle = jnp.asarray(high), jnp.asarray(low), jnp.asarray(shuffle)
    owners = jnp.arange(tile_count, dtype=jnp.int32)
    reads = lookup(owner_map, tile_of)[None, :] == owners[:, None]
    which = jnp.sum(jnp.where(reads, jnp.arange(pos_dev, dtype=jnp.int32), 0), axis=1)
    notes = jnp.stack(
        [jnp.any(reads, axis=1).astype(jnp.int32)]
        + [jnp.sum(jnp.where(reads, offsets[:, axis], 0), axis=1) for axis in range(2)],
        axis=1,
    )
    notes = lax.all_to_all(notes, "tile", split_axis=0, concat_axis=0, tiled=True)
    notes, which = lax.optimization_barrier((notes, which))
    arrived = lax.all_to_all(spread(which, patterns), "tile", split_axis=0, concat_axis=0, tiled=True)
    present = notes[:, 0] > 0
    rank = jnp.sum(jnp.where((owners[None, :] < owners[:, None]) & present[None, :], 1, 0), axis=1)
    chosen = (rank[None, :] == jnp.arange(MAX_READS, dtype=jnp.int32)[:, None]) & present[None, :]
    info = jnp.stack([owners, notes[:, 1], notes[:, 2]])
    info = jnp.sum(jnp.where(chosen[None], info[:, None, :], 0), axis=2).reshape(-1)
    info = jnp.concatenate([info, jnp.sum(notes[:, 0])[None]])
    tile = object_tiles[0]
    back, far = forward(info, tile, probe_wave, high, low)
    tile_grad, probe_part = backward(
        info, tile, probe_wave, high, low, shuffle, back, far, arrived
    )
    object_part = lax.psum_scatter(tile_grad, "scan", scatter_dimension=3, tiled=True)
    probe_total = lax.psum(probe_part, ("scan", "tile"))
    count = tile_count * lax.axis_size("scan") * pos_dev
    return object_part, probe_total / jnp.sqrt(jnp.ones((), F32) * count)


def solution(mesh):
    return jax.shard_map(
        per_device,
        mesh=mesh,
        in_specs=(
            P("tile", None, None, None, None),
            P(),
            P(("scan", "tile"), None, None),
            P(("scan", "tile")),
            P(("scan", "tile"), None),
            P(),
        ),
        out_specs=(P("tile", None, None, "scan", None), P()),
        check_vma=False,
    )
```

time: 1070 us -> 271 us (0.25); the launches traced: 1050 us -> 270 us
  local copies, waits for them, and re-layouts: 295 us -> 1.04 us
  waiting for transfers between devices: 466 us -> 195 us
  matrix products: 117 us -> 0 us
  loops' own time: 56.8 us -> 0 us
  other arithmetic: 54.3 us -> 5.09 us
  Pallas kernels: 0 us -> 34.3 us
  blocking collectives: 29.9 us -> 13.8 us
    all_to_all x2 -> x1, waiting for transfers between devices: 419 us -> 37.2 us  [per_device(): lax.all_to_all(spread(which, patterns), 'tile', split_axis=0, concat_axis...]
    dynamic_update_slice x16 -> x0, local copies, waits for them, and re-layouts: 175 us -> none  [add_one(): return lax.dynamic_update_slice(running, current + grads[slot_index], start)]
    psum x1, waiting for transfers between devices: 0.02 us -> 158 us  [per_device(): probe_total = lax.psum(probe_part, ('scan', 'tile'))]
    dot_general x49 -> x0, matrix products: 117 us -> none  [the longest x48 108 us: real_product(): jnp.dot(left, right, precision=lax.Precision.HIGHEST, preferred_element_t...]
    gather x49 -> x0, local copies, waits for them, and re-layouts: 85.3 us -> none
    another operation x2 -> x0, loops' own time: 56.8 us -> none  [the longest x1 56.8 us: accumulate(): return lax.fori_loop(0, grads.shape[0], add_one, total)]
    reduce_scatter x1, waiting for transfers between devices: 46.8 us -> 0.01 us  [per_device(): lax.psum_scatter(tile_grad, 'scan', scatter_dimension=3, tiled=True)]
    pallas_call x0 -> x3, Pallas kernels: none -> 34.3 us  [the longest x1 17.6 us: backward(): pl.pallas_call(backward_kernel, out_shape=(grad, probe_grad), grid_spec=p...]
  transfers between devices with their start and end apart: 4 -> 3, of which waited for: 3 -> 2; matrix products, arithmetic and copies ran while one was open for 21% -> 1% of each run, Pallas kernels for 0% -> 5%
where the time goes in v1:
time: 271 us; the launch traced here: 270 us
  waiting for transfers between devices  195 us (72%)
  Pallas kernels  34.3 us (13%)
  between operations  15.5 us (6%)
  blocking collectives  13.8 us (5%)
  other arithmetic  5.09 us (2%)
  starting transfers between devices  4.76 us (2%)
    psum x1, waiting for transfers between devices, per_device(): probe_total = lax.psum(probe_part, ('scan', 'tile'))  158 us
    all_to_all x1, waiting for transfers between devices, per_device(): lax.all_to_all(spread(which, patterns), 'tile', split_axis=0, concat_axis...  37.2 us
    pallas_call x1, Pallas kernels, backward(): pl.pallas_call(backward_kernel, out_shape=(grad, probe_grad), grid_spec=p...  17.6 us
    all_to_all x1, blocking collectives, per_device(): lax.all_to_all(notes, 'tile', split_axis=0, concat_axis=0, tiled=True)  13.8 us
    pallas_call x1, Pallas kernels, forward(): pl.pallas_call(forward_kernel, out_shape=(out, out), grid_spec=pltpu.Pref...  12.8 us
  transfers between devices with their start and end apart: 3, of which 2 were waited for; matrix products, arithmetic and copies ran while one was open for 1% of the time, Pallas kernels for 5%

profile of v1, /device:TPU:1, one launch (start us, length us, event | category | flops | bytes accessed | tf_op | source)
XLA Modules:
  0.0 270.0 jit_solution(2630429561620885731)
XLA Ops:
  8.0 0.9 select_reduce_fusion.5
  8.9 0.1 fusion.2
  8.9 0.8 slice_bitcast_fusion.3
  9.7 0.6 select_reduce_fusion.2
  10.3 0.1 copy.13
  10.4 13.8 %all_to_all.17 = s32[16,1,3]{2,1,0:T(1,128)S(1)} all-to-all(s32[16,1,3]{2,1,0:T(1,128)S(1)} %copy.13), channel_id=1, replica_groups=mesh['scan'=8,'tile'=16] {'tile'}, dimensions={0} | all-to-all | bytes 384 | tf_op jit(solution)/shard_map/all_to_all | solution.py:339
  24.2 0.1 copy.14
  24.3 4.0 %shard_map.105 = f32[16,256,256]{2,1,0:T(8,128)} custom-call(s32[16]{0:T(128)} %get-tuple-element.11.which, f32[4,256,256]{2,1,0:T(8,128)} %patterns.1), custom_call_target="tpu_custom_call" | custom-call | tf_op jit(solution)/shard_map/pallas_call | solution.py:308
  28.3 0.0 copy-start
  28.3 0.0 copy-start.1
  28.3 0.0 copy-start.2
  28.3 4.7 %all-to-all-start.1 = ((f32[16,256,256]{2,1,0:T(8,128)}), f32[16,256,256]{2,1,0:T(8,128)}, u32[]{:S(2)}, u32[]{:S(2)}) async-start(f32[16,256,256]{2,1,0:T(8,128)} %shard_map.105), calls=%async_computation.1 | async-start | bytes 8388608 | tf_op jit(solution)/shard_map/all_to_all | solution.py:341
  33.0 0.0 all-reduce.2.cloned.1.call-start
  33.0 0.6 slice_bitcast_fusion.1
  33.7 0.1 select_reduce_fusion.1
  33.8 0.1 select_reduce_fusion
  34.0 0.1 reshape.64
  34.0 0.7 pad_add_fusion.1.info
  34.8 0.0 copy-done
  34.8 0.0 copy-done.1
  34.8 0.0 copy-done.2
  34.8 0.0 copy-start.3
  34.8 12.8 %shard_map.104 = (f32[8,2,256,256]{3,2,1,0:T(8,128)}, f32[8,2,256,256]{3,2,1,0:T(8,128)}) custom-call(s32[25]{0:T(128)S(1)} %pad_add_fusion.1.info, f32[2,2,512,512]{3,2,1,0:T(8,128)} %bitcast.23, f32[2,256,256]{2,1,0:T(8,128)S(1)} %copy-done, bf16[8,256,256]{2,1,0:T(8,128)(2,1)S(1)} %copy-done.2, bf16[8,256,256]{2,1,0:T(8,128)(2,1)S(1)} %copy-done.1), custom_call_target="tpu_custom_call" | custom-call | flops 6442450944 | bytes 14680064 | tf_op jit(solution)/shard_map/pallas_call | solution.py:255
  47.5 37.2 %all-to-all-done.1.pattern = f32[16,256,256]{2,1,0:T(8,128)} async-done(((f32[16,256,256]{2,1,0:T(8,128)}), f32[16,256,256]{2,1,0:T(8,128)}, u32[]{:S(2)}, u32[]{:S(2)}) %all-to-all-start.1) | async-done | bytes 4194336 | tf_op jit(solution)/shard_map/all_to_all | solution.py:341
  84.8 0.0 copy-done.3
  84.8 17.6 %shard_map.106 = (f32[1,2,2,512,512]{4,3,2,1,0:T(8,128)}, f32[2,256,256]{2,1,0:T(8,128)}) custom-call(s32[25]{0:T(128)S(1)} %pad_add_fusion.1.info, f32[2,2,512,512]{3,2,1,0:T(8,128)} %bitcast.24, f32[2,256,256]{2,1,0:T(8,128)S(1)} %copy-done, bf16[8,256,256]{2,1,0:T(8,128)(2,1)S(1)} %copy-done.2, bf16[8,256,256]{2,1,0:T(8,128)(2,1)S(1)} %copy-done.1, ...), custom_call_target="tpu_custom_call" | custom-call | flops 6979321856 | bytes 20971520 | tf_op jit(solution)/shard_map/pallas_call | solution.py:277
  102.4 0.0 all-reduce.2.cloned.1.call-update
  102.4 0.0 reduce-scatter.2.cloned.1.call-start
  102.5 0.5 reduce-scatter.2.cloned.1.call-update
  103.0 157.7 %all-reduce.2.cloned.1.call-done = f32[2,256,256]{2,1,0:T(8,128)} async-done(((f32[2,256,256]{2,1,0:T(8,128)}), f32[2,256,256]{2,1,0:T(8,128)}) %all-reduce.2.cloned.1.call-update) | async-done | bytes 524304 | tf_op jit(solution)/shard_map/psum | solution.py:354
  260.7 1.9 broadcast_multiply_fusion
  262.5 0.0 reduce-scatter.2.cloned.1.call-done
  (6 shorter events, 0.0 us)
Async XLA Ops:
  28.3 6.5 %copy-start = (f32[2,256,256]{2,1,0:T(8,128)S(1)}, f32[2,256,256]{2,1,0:T(8,128)}, u32[]{:S(2)}) copy-start(f32[2,256,256]{2,1,0:T(8,128)} %probe.3) | copy-start | bytes 1572868
  28.3 6.5 %copy-start.1 = (bf16[8,256,256]{2,1,0:T(8,128)(2,1)S(1)}, bf16[8,256,256]{2,1,0:T(8,128)(2,1)}, u32[]{:S(2)}) copy-start(bf16[8,256,256]{2,1,0:T(8,128)(2,1)} %constant.17.clone.lo) | copy-start | bytes 3145732
  28.3 6.5 %copy-start.2 = (bf16[8,256,256]{2,1,0:T(8,128)(2,1)S(1)}, bf16[8,256,256]{2,1,0:T(8,128)(2,1)}, u32[]{:S(2)}) copy-start(bf16[8,256,256]{2,1,0:T(8,128)(2,1)} %constant.16.clone.hi) | copy-start | bytes 3145732
  28.3 56.5 %all-to-all-start.1 = ((f32[16,256,256]{2,1,0:T(8,128)}), f32[16,256,256]{2,1,0:T(8,128)}, u32[]{:S(2)}, u32[]{:S(2)}) async-start(f32[16,256,256]{2,1,0:T(8,128)} %shard_map.105), calls=%async_computation.1 | async-start | bytes 8388608 | tf_op jit(solution)/shard_map/all_to_all | solution.py:341
  33.0 227.7 %all-reduce.2.cloned.1.call-start = ((), (), s32[]{:S(2)}) async-start(), calls=%async_computation.4 | async-start | bytes 1048576 | tf_op jit(solution)/shard_map/psum | solution.py:354
  34.8 50.0 %copy-start.3 = (bf16[256,256]{1,0:T(8,128)(2,1)S(1)}, bf16[256,256]{1,0:T(8,128)(2,1)}, u32[]{:S(2)}) copy-start(bf16[256,256]{1,0:T(8,128)(2,1)} %constant.18.clone.shuffle) | copy-start | bytes 393220
  102.4 160.1 %reduce-scatter.2.cloned.1.call-start = ((), (), s32[]{:S(2)}) async-start(), calls=%async_computation.3 | async-start | bytes 4718592 | tf_op jit(solution)/shard_map/reduce_scatter | solution.py:353
Sparse Core Ops, SparseCore 0:
  102.5 158.0 all-reduce.1
Sparse Core Ops, SparseCore 1:
  105.9 43.2 reduce-scatter.1

commit v2 on v1

--- a/solution.py
+++ b/solution.py
@@ -318,6 +318,157 @@
     )(which, patterns)
 
 
+MESH = pl.DeviceIdType.MESH
+CORES = 2
+
+
+def reduce_kernel(
+    zs, xs, ys, grad, probe, out, probe_out,
+    own, core_in, half_in, direct_in, plane_in, piece_in, piece_z,
+    load_sem, core_send, core_recv, ring_send, ring_recv, probe_send, probe_recv, z_send, z_recv,
+    all_send, all_recv, pair_send, pair_recv,
+):
+    scan, tile = lax.axis_index("scan"), lax.axis_index("tile")
+    z, c = scan // CORES, scan % CORES
+    x, y = tile // ys, tile % ys
+    height = out.shape[3]
+    piece = piece_z.shape[1]
+
+    def at_z(step):
+        return {"scan": lax.rem(z + step + zs, zs) * CORES + c}
+
+    def at_xy(j):
+        return {"tile": lax.rem(x + j // ys, xs) * ys + lax.rem(y + j % ys, ys)}
+
+    pair = {"scan": z * CORES + 1 - c}
+    shifts = range(1, xs * ys)
+    steps = [2, 1, -1, 0]
+
+    def rows_of(step, core):
+        return pl.ds(pl.multiple_of((lax.rem(z + step + zs, zs) * CORES + core) * height, height), height)
+
+    barrier = pltpu.get_barrier_semaphore()
+    partners = [pair] + [at_z(step) for step in (1, 2, 3)] + [at_xy(j) for j in shifts]
+    for partner in partners:
+        pl.semaphore_signal(barrier, inc=1, device_id=partner, device_id_type=MESH)
+    loads = [
+        pltpu.make_async_copy(grad.at[0, :, :, rows_of(step, c), :], own.at[k], load_sem.at[k])
+        for k, step in enumerate(steps)
+    ]
+    for load in loads:
+        load.start()
+    pl.semaphore_wait(barrier, len(partners))
+
+    def remote(src, dst, send, recv, device):
+        return pltpu.make_async_remote_copy(
+            src_ref=src, dst_ref=dst, send_sem=send, recv_sem=recv, device_id=device, device_id_type=MESH
+        )
+
+    started = []
+
+    def go(copy):
+        copy.start()
+        started.append(copy)
+        return copy
+
+    probe_pair = go(remote(probe.at[1 - c], plane_in, core_send.at[4], core_recv.at[4], pair))
+    cores = [
+        go(remote(grad.at[0, :, :, rows_of(step, 1 - c), :], core_in.at[k], core_send.at[k], core_recv.at[k], pair))
+        for k, step in enumerate(steps)
+    ]
+
+    def merge(k):
+        loads[k].wait()
+        cores[k].wait_recv()
+        own[k] = own[k] + core_in[k]
+
+    merge(0)
+    halves = [
+        go(remote(own.at[0, 0], half_in.at[0], ring_send.at[0], ring_recv.at[0], at_z(1))),
+        go(remote(own.at[0, 1], half_in.at[1], ring_send.at[1], ring_recv.at[1], at_z(-1))),
+    ]
+    probe_pair.wait_recv()
+    plane_in[...] = plane_in[...] + probe[c]
+
+    def piece_rows(device):
+        return pl.ds(pl.multiple_of(device["tile"] * piece, piece), piece)
+
+    gathers = [
+        go(remote(plane_in.at[piece_rows(at_xy(j))], piece_in.at[j], probe_send.at[j], probe_recv.at[j], at_xy(j)))
+        for j in shifts
+    ]
+    merge(1)
+    up = go(remote(own.at[1, 1], direct_in.at[0], ring_send.at[2], ring_recv.at[2], at_z(1)))
+    merge(2)
+    down = go(remote(own.at[2, 0], direct_in.at[1], ring_send.at[3], ring_recv.at[3], at_z(-1)))
+    halves[0].wait_recv()
+    own[1, 0] = own[1, 0] + half_in[0]
+    up_sum = go(remote(own.at[1, 0], direct_in.at[2], ring_send.at[4], ring_recv.at[4], at_z(1)))
+    halves[1].wait_recv()
+    own[2, 1] = own[2, 1] + half_in[1]
+    down_sum = go(remote(own.at[2, 1], direct_in.at[3], ring_send.at[5], ring_recv.at[5], at_z(-1)))
+
+    total = plane_in[piece_rows({"tile": tile}), :]
+    for copy, j in zip(gathers, shifts):
+        copy.wait_recv()
+        total = total + piece_in[j]
+    piece_z[0] = total
+    across = [go(remote(piece_z.at[0], piece_z.at[k], z_send.at[k], z_recv.at[k], at_z(k))) for k in (1, 2, 3)]
+    merge(3)
+    for copy in across:
+        copy.wait_recv()
+    mine = piece_rows({"tile": tile})
+    probe_out[c, mine, :] = (piece_z[0] + piece_z[1]) + (piece_z[2] + piece_z[3])
+    spreads = [
+        go(remote(probe_out.at[c, mine], probe_out.at[c, mine], all_send.at[j], all_recv.at[j], at_xy(j)))
+        for j in shifts
+    ]
+    for copy in spreads:
+        copy.wait_recv()
+    last = go(remote(probe_out.at[c], probe_out.at[c], pair_send, pair_recv, pair))
+    up.wait_recv()
+    down.wait_recv()
+    up_sum.wait_recv()
+    down_sum.wait_recv()
+    out[0, 0] = own[3, 0] + (direct_in[2] + direct_in[1])
+    out[0, 1] = own[3, 1] + (direct_in[0] + direct_in[3])
+    last.wait_recv()
+    for copy in started:
+        copy.wait_send()
+
+
+def reduce_all(sizes, grad, probe):
+    zs, xs, ys = sizes
+    tiles = xs * ys
+    slices, comps, side, width = grad.shape[1:]
+    height = side // (zs * CORES)
+    piece = SIDE // tiles
+    dma = pltpu.SemaphoreType.DMA
+    return pl.pallas_call(
+        functools.partial(reduce_kernel, zs, xs, ys),
+        out_shape=(
+            jax.ShapeDtypeStruct((1, slices, comps, height, width), F32),
+            jax.ShapeDtypeStruct(probe.shape, F32),
+        ),
+        in_specs=[pl.BlockSpec(memory_space=pl.ANY), pl.BlockSpec(memory_space=pltpu.VMEM)],
+        out_specs=(pl.BlockSpec(memory_space=pltpu.VMEM),) * 2,
+        scratch_shapes=[
+            pltpu.VMEM((4, slices, comps, height, width), F32),
+            pltpu.VMEM((4, slices, comps, height, width), F32),
+            pltpu.VMEM((2, comps, height, width), F32),
+            pltpu.VMEM((4, comps, height, width), F32),
+            pltpu.VMEM((SIDE, SIDE), F32),
+            pltpu.VMEM((tiles, piece, SIDE), F32),
+            pltpu.VMEM((4, piece, SIDE), F32),
+            dma((4,)), dma((5,)), dma((5,)), dma((6,)), dma((6,)), dma((tiles,)), dma((tiles,)),
+            dma((4,)), dma((4,)), dma((tiles,)), dma((tiles,)), dma, dma,
+        ],
+        compiler_params=pltpu.CompilerParams(
+            collective_id=1, has_side_effects=True, vmem_limit_bytes=32 << 20
+        ),
+    )(grad, probe)
+
+
 def lookup(table, indices):
     choices = jnp.arange(table.shape[0], dtype=jnp.int32)
     return jnp.sum(jnp.where(indices[..., None] == choices, table, 0), axis=-1)
@@ -350,8 +501,8 @@
     tile_grad, probe_part = backward(
         info, tile, probe_wave, high, low, shuffle, back, far, arrived
     )
-    object_part = lax.psum_scatter(tile_grad, "scan", scatter_dimension=3, tiled=True)
-    probe_total = lax.psum(probe_part, ("scan", "tile"))
+    zs, xs = lax.axis_size("scan") // CORES, math.isqrt(tile_count)
+    object_part, probe_total = reduce_all((zs, xs, tile_count // xs), tile_grad, probe_part)
     count = tile_count * lax.axis_size("scan") * pos_dev
     return object_part, probe_total / jnp.sqrt(jnp.ones((), F32) * count)
 

time: 271 us -> 143 us (0.53)
  waiting for transfers between devices: 195 us -> 38.4 us
  Pallas kernels: 34.3 us -> 76.4 us
  between operations: 15.5 us -> 0.7 us
  local copies, waits for them, and re-layouts: 1.04 us -> 4.02 us
    psum x1 -> x0, waiting for transfers between devices: 158 us -> none  [per_device(): probe_total = lax.psum(probe_part, ('scan', 'tile'))]
    pallas_call x0 -> x1, Pallas kernels: none -> 45.1 us  [reduce_all(): pl.pallas_call(functools.partial(reduce_kernel, zs, xs, ys), out_shape=(j...]
    unnamed x8 -> x11, local copies, waits for them, and re-layouts: 0.02 us -> 3 us
  transfers between devices with their start and end apart: 3 -> 1, of which waited for: 2 -> 1; matrix products, arithmetic and copies ran while one was open for 1% -> 1% of each run, Pallas kernels for 5% -> 8%
where the time goes in v2:
time: 143 us; the launch traced here: 142 us
  Pallas kernels  76.4 us (53%)
  waiting for transfers between devices  38.4 us (27%)
  blocking collectives  13.8 us (10%)
  starting transfers between devices  4.68 us (3%)
  other arithmetic  4.05 us (3%)
  local copies, waits for them, and re-layouts  4.02 us (3%)
    pallas_call x1, Pallas kernels, reduce_all(): pl.pallas_call(functools.partial(reduce_kernel, zs, xs, ys), out_shape=(j...  45.1 us
    all_to_all x1, waiting for transfers between devices, per_device(): lax.all_to_all(spread(which, patterns), 'tile', split_axis=0, concat_axis...  38.4 us
    pallas_call x1, Pallas kernels, backward(): pl.pallas_call(backward_kernel, out_shape=(grad, probe_grad), grid_spec=p...  15.7 us
    all_to_all x1, blocking collectives, per_device(): lax.all_to_all(notes, 'tile', split_axis=0, concat_axis=0, tiled=True)  13.8 us
    pallas_call x1, Pallas kernels, forward(): pl.pallas_call(forward_kernel, out_shape=(out, out), grid_spec=pltpu.Pref...  11.6 us
    all_to_all x1, starting transfers between devices, per_device(): lax.all_to_all(spread(which, patterns), 'tile', split_axis=0, concat_axis...  4.68 us
    pallas_call x1, Pallas kernels, spread(): pl.pallas_call(spread_kernel, out_shape=jax.ShapeDtypeStruct((count,) + p...  4 us
    unnamed x11, local copies, waits for them, and re-layouts  3 us
  transfers between devices with their start and end apart: 1, of which 1 were waited for; matrix products, arithmetic and copies ran while one was open for 1% of the time, Pallas kernels for 8%

profile of v2, /device:TPU:1, one launch (start us, length us, event | category | flops | bytes accessed | tf_op | source)
XLA Modules:
  0.0 142.1 jit_solution(10872583657886035374)
XLA Ops:
  0.6 0.9 select_reduce_fusion.5
  1.5 0.1 fusion.2
  1.6 0.8 slice_bitcast_fusion.3
  2.3 0.6 select_reduce_fusion.2
  2.9 0.1 copy.13
  3.0 13.8 %all_to_all.17 = s32[16,1,3]{2,1,0:T(1,128)S(1)} all-to-all(s32[16,1,3]{2,1,0:T(1,128)S(1)} %copy.13), channel_id=1, replica_groups=mesh['scan'=8,'tile'=16] {'tile'}, dimensions={0} | all-to-all | bytes 384 | tf_op jit(solution)/shard_map/all_to_all | solution.py:490
  16.8 0.1 copy.14
  16.9 4.0 %shard_map.105 = f32[16,256,256]{2,1,0:T(8,128)} custom-call(s32[16]{0:T(128)} %get-tuple-element.13.which, f32[4,256,256]{2,1,0:T(8,128)} %patterns.1), custom_call_target="tpu_custom_call" | custom-call | tf_op jit(solution)/shard_map/pallas_call | solution.py:308
  20.9 0.0 copy-start.1
  20.9 0.0 copy-start.2
  20.9 0.0 copy-start.3
  21.0 4.7 %all-to-all-start.1 = ((f32[16,256,256]{2,1,0:T(8,128)}), f32[16,256,256]{2,1,0:T(8,128)}, u32[]{:S(2)}, u32[]{:S(2)}) async-start(f32[16,256,256]{2,1,0:T(8,128)} %shard_map.105), calls=%async_computation.1 | async-start | bytes 8388608 | tf_op jit(solution)/shard_map/all_to_all | solution.py:492
  25.6 0.6 slice_bitcast_fusion.1
  26.3 0.1 select_reduce_fusion.1
  26.4 0.1 select_reduce_fusion
  26.6 0.1 reshape.64
  26.7 0.7 pad_add_fusion.1.info
  27.4 0.0 copy-done.1
  27.4 0.0 copy-done.2
  27.4 0.0 copy-done.3
  27.4 0.0 copy-start.4
  27.4 11.6 %shard_map.104 = (f32[8,2,256,256]{3,2,1,0:T(8,128)}, f32[8,2,256,256]{3,2,1,0:T(8,128)}) custom-call(s32[25]{0:T(128)S(1)} %pad_add_fusion.1.info, f32[2,2,512,512]{3,2,1,0:T(8,128)} %bitcast.23, f32[2,256,256]{2,1,0:T(8,128)S(1)} %copy-done.1, bf16[8,256,256]{2,1,0:T(8,128)(2,1)S(1)} %copy-done.3, bf16[8,256,256]{2,1,0:T(8,128)(2,1)S(1)} %copy-done.2), custom_call_target="tpu_custom_call" | custom-call | flops 6442450944 | bytes 14680064 | tf_op jit(solution)/shard_map/pallas_call | solution.py:255
  39.0 38.4 %all-to-all-done.1.pattern = f32[16,256,256]{2,1,0:T(8,128)} async-done(((f32[16,256,256]{2,1,0:T(8,128)}), f32[16,256,256]{2,1,0:T(8,128)}, u32[]{:S(2)}, u32[]{:S(2)}) %all-to-all-start.1) | async-done | bytes 4194336 | tf_op jit(solution)/shard_map/all_to_all | solution.py:492
  77.4 0.0 copy-done.4
  77.4 15.7 %shard_map.106 = (f32[1,2,2,512,512]{4,3,2,1,0:T(8,128)}, f32[2,256,256]{2,1,0:T(8,128)S(1)}) custom-call(s32[25]{0:T(128)S(1)} %pad_add_fusion.1.info, f32[2,2,512,512]{3,2,1,0:T(8,128)} %bitcast.24, f32[2,256,256]{2,1,0:T(8,128)S(1)} %copy-done.1, bf16[8,256,256]{2,1,0:T(8,128)(2,1)S(1)} %copy-done.3, bf16[8,256,256]{2,1,0:T(8,128)(2,1)S(1)} %copy-done.2, ...), custom_call_target="tpu_custom_call" | custom-call | flops 6979321856 | bytes 20971520 | tf_op jit(solution)/shard_map/pallas_call | solution.py:277
  93.1 0.0 copy-start
  93.1 2.2 %copy-done = f32[1,2,2,512,512]{4,3,2,1,0:T(8,128)S(1)} copy-done((f32[1,2,2,512,512]{4,3,2,1,0:T(8,128)S(1)}, f32[1,2,2,512,512]{4,3,2,1,0:T(8,128)}, u32[]{:S(2)}) %copy-start) | copy-done | bytes 4194328
  95.3 45.1 %shard_map.107 = (f32[1,2,2,64,512]{4,3,2,1,0:T(8,128)S(1)}, f32[2,256,256]{2,1,0:T(8,128)S(1)}) custom-call(f32[1,2,2,512,512]{4,3,2,1,0:T(8,128)S(1)} %copy-done, f32[2,256,256]{2,1,0:T(8,128)S(1)} %get-tuple-element.15.probe), custom_call_target="tpu_custom_call" | custom-call | tf_op jit(solution)/shard_map/pallas_call | solution.py:447
  140.4 0.8 broadcast_multiply_fusion
  141.3 0.8 copy.16
  (6 shorter events, 0.0 us)
Async XLA Ops:
  20.9 6.5 %copy-start.1 = (f32[2,256,256]{2,1,0:T(8,128)S(1)}, f32[2,256,256]{2,1,0:T(8,128)}, u32[]{:S(2)}) copy-start(f32[2,256,256]{2,1,0:T(8,128)} %probe.3) | copy-start | bytes 1572868
  20.9 6.5 %copy-start.2 = (bf16[8,256,256]{2,1,0:T(8,128)(2,1)S(1)}, bf16[8,256,256]{2,1,0:T(8,128)(2,1)}, u32[]{:S(2)}) copy-start(bf16[8,256,256]{2,1,0:T(8,128)(2,1)} %constant.17.clone.lo) | copy-start | bytes 3145732
  20.9 6.5 %copy-start.3 = (bf16[8,256,256]{2,1,0:T(8,128)(2,1)S(1)}, bf16[8,256,256]{2,1,0:T(8,128)(2,1)}, u32[]{:S(2)}) copy-start(bf16[8,256,256]{2,1,0:T(8,128)(2,1)} %constant.16.clone.hi) | copy-start | bytes 3145732
  21.0 56.5 %all-to-all-start.1 = ((f32[16,256,256]{2,1,0:T(8,128)}), f32[16,256,256]{2,1,0:T(8,128)}, u32[]{:S(2)}, u32[]{:S(2)}) async-start(f32[16,256,256]{2,1,0:T(8,128)} %shard_map.105), calls=%async_computation.1 | async-start | bytes 8388608 | tf_op jit(solution)/shard_map/all_to_all | solution.py:492
  27.4 50.0 %copy-start.4 = (bf16[256,256]{1,0:T(8,128)(2,1)S(1)}, bf16[256,256]{1,0:T(8,128)(2,1)}, u32[]{:S(2)}) copy-start(bf16[256,256]{1,0:T(8,128)(2,1)} %constant.18.clone.shuffle) | copy-start | bytes 393220
  93.1 2.2 %copy-start = (f32[1,2,2,512,512]{4,3,2,1,0:T(8,128)S(1)}, f32[1,2,2,512,512]{4,3,2,1,0:T(8,128)}, u32[]{:S(2)}) copy-start(f32[1,2,2,512,512]{4,3,2,1,0:T(8,128)} %get-tuple-element.14.grad) | copy-start | bytes 12582916

commit v3 on v2

--- a/solution.py
+++ b/solution.py
@@ -169,48 +169,204 @@
             ]
 
 
-def close_tile(held, grad):
-    for plane in range(4):
-        for k in range(4):
-            grad[0, plane // 2, plane % 2, :, k * HALF : (k + 1) * HALF] = held[
-                plane, pl.ds(k, 2 * SIDE, stride=4), :
-            ]
-
-
-def forward_kernel(info, tile, probe, hi, lo, back, far, held):
-    k = pl.program_id(0)
-
-    @pl.when(k == 0)
-    def _():
-        open_tile(tile, held)
-
-    @pl.when(k < info[3 * MAX_READS])
-    def _():
-        a, b = info[MAX_READS + k], info[2 * MAX_READS + k]
-        ore, oim = patch(held.at[0], a, b), patch(held.at[1], a, b)
-        pre, pim = probe[0], probe[1]
-        re, im = travel(pre * ore - pim * oim, pre * oim + pim * ore, hi, lo, False)
-        back[0, 0], back[0, 1] = re, im
-        ore, oim = patch(held.at[2], a, b), patch(held.at[3], a, b)
-        far[0, 0], far[0, 1] = to_far(re * ore - im * oim, re * oim + im * ore, hi, lo)
+def forward_one(a, b, held, probe, hi, lo):
+    ore, oim = patch(held.at[0], a, b), patch(held.at[1], a, b)
+    pre, pim = probe[0], probe[1]
+    back = travel(pre * ore - pim * oim, pre * oim + pim * ore, hi, lo, False)
+    ore, oim = patch(held.at[2], a, b), patch(held.at[3], a, b)
+    re, im = back
+    return back, to_far(re * ore - im * oim, re * oim + im * ore, hi, lo)
+
+
+MESH = pl.DeviceIdType.MESH
+CORES = 2
+
+
+def remote(src, dst, send, recv, device):
+    return pltpu.make_async_remote_copy(
+        src_ref=src, dst_ref=dst, send_sem=send, recv_sem=recv, device_id=device, device_id_type=MESH
+    )
+
+
+def plane_steps(xs, ys):
+    tile = lax.axis_index("tile")
+    x, y = tile // ys, tile % ys
+
+    def at_xy(j):
+        return {"tile": lax.rem(x + j // ys, xs) * ys + lax.rem(y + j % ys, ys)}
+
+    return tile, at_xy, range(1, xs * ys)
+
+
+def read_lists(notes, tables_ref):
+    count = notes.shape[0]
+    note = notes[:, 0, :]
+    owner = lax.broadcasted_iota(jnp.int32, note.shape, 1)
+    source = lax.broadcasted_iota(jnp.int32, note.shape, 0)
+    here = jnp.zeros(note.shape, jnp.int32)
+    values = [jnp.zeros(note.shape, jnp.int32) for _ in range(3)]
+    for i in range(4):
+        hit = jnp.where(jnp.broadcast_to(note[:, i : i + 1], note.shape) == owner, 1, 0)
+        here = here + hit
+        fields = [4 * source + i] + [
+            jnp.broadcast_to(note[:, 4 * f + i : 4 * f + i + 1], note.shape) for f in (1, 2)
+        ]
+        values = [v + hit * f for v, f in zip(values, fields)]
+    lower = (
+        lax.broadcasted_iota(jnp.int32, (count, count), 0) > lax.broadcasted_iota(jnp.int32, (count, count), 1)
+    ).astype(F32)
+    rank = mm(lower.astype(BF16), here.astype(F32).astype(BF16)).astype(jnp.int32)
+    for k in range(MAX_READS):
+        chosen = here * jnp.where(rank == k, 1, 0)
+        for f in range(3):
+            row = MAX_READS * f + k
+            tables_ref[row : row + 1, :] = jnp.sum(chosen * values[f], axis=0, keepdims=True)
+    tables_ref[24:25, :] = jnp.sum(here, axis=0, keepdims=True)
+
+
+def exchange_kernel(
+    xs, ys, tile_of, offsets, owner_map, patterns, tile, probe_hbm, hi_hbm, lo_hbm,
+    held, arrived, back, far, info,
+    opened, probe, hi, lo, notes, lists, lists_smem, mid, stage,
+    load_sem, own_sem, list_sem, note_send, note_recv, first_send, first_recv, second_send, second_recv,
+):
+    me, at_xy, shifts = plane_steps(xs, ys)
+    piece = mid.shape[1]
+    reads = patterns.shape[0]
+
+    def piece_rows(index):
+        return pl.ds(pl.multiple_of(index * piece, piece), piece)
+
+    barrier = pltpu.get_barrier_semaphore()
+    for j in shifts:
+        pl.semaphore_signal(barrier, inc=1, device_id=at_xy(j), device_id_type=MESH)
+    loads = [
+        pltpu.make_async_copy(src, dst, load_sem.at[k])
+        for k, (src, dst) in enumerate(
+            [(tile, opened), (probe_hbm, probe), (hi_hbm, hi), (lo_hbm, lo)]
+        )
+    ]
+    for load in loads:
+        load.start()
+    own = pltpu.make_async_copy(
+        patterns.at[:, piece_rows(me), :], mid.at[pl.ds(reads * me, reads)], own_sem
+    )
+    own.start()
+    lane = lax.broadcasted_iota(jnp.int32, (1, HALF), 1)
+    note = jnp.zeros((1, HALF), jnp.int32)
+    for i in range(reads):
+        for f, value in enumerate((owner_map[tile_of[i]], offsets[i, 0], offsets[i, 1])):
+            note = jnp.where(lane == 4 * f + i, value, note)
+    notes[me] = note
+    pl.semaphore_wait(barrier, len(shifts))
+
+    tells = [
+        remote(notes.at[me], notes.at[me], note_send.at[j], note_recv.at[j], at_xy(j)) for j in shifts
+    ]
+    firsts = [
+        remote(
+            patterns.at[:, piece_rows(at_xy(j)["tile"]), :], mid.at[pl.ds(reads * me, reads)],
+            first_send.at[j], first_recv.at[j], at_xy(j),
+        )
+        for j in shifts
+    ]
+    for copy in tells + firsts:
+        copy.start()
+    loads[0].wait()
+    open_tile(opened.at[0], held)
+    for copy in tells:
+        copy.wait_recv()
+    lists[...] = jnp.zeros_like(lists)
+    read_lists(notes, lists)
+    listed = pltpu.make_async_copy(lists, lists_smem, list_sem)
+    listed.start()
+    listed.wait()
+    for row in range(3):
+        for k in range(MAX_READS):
+            info[row, k] = lists_smem[MAX_READS * row + k, me]
+    for k in range(MAX_READS):
+        info[3, k] = lists_smem[24, me]
+    own.wait()
+    for copy in firsts:
+        copy.wait_recv()
+    seconds = []
+    for j in shifts:
+        to = at_xy(j)["tile"]
+        for k in range(MAX_READS):
+            stage[j, k] = mid[lists_smem[k, to]]
+        copy = remote(
+            stage.at[j], arrived.at[:, piece_rows(me), :], second_send.at[j], second_recv.at[j], at_xy(j)
+        )
+        copy.start()
+        seconds.append(copy)
+    for k in range(MAX_READS):
+        arrived[k, piece_rows(me), :] = mid[lists_smem[k, me]]
+    for load in loads[1:]:
+        load.wait()
+
+    def one(k, carry):
+        a, b = lists_smem[MAX_READS + k, me], lists_smem[2 * MAX_READS + k, me]
+        (bre, bim), (fre, fim) = forward_one(a, b, held, probe, hi, lo)
+        back[k, 0], back[k, 1], far[k, 0], far[k, 1] = bre, bim, fre, fim
+        return carry
+
+    lax.fori_loop(0, MAX_READS, one, 0)
+    for copy in seconds:
+        copy.wait_recv()
+    for copy in tells + firsts + seconds:
+        copy.wait_send()
+
+
+def exchange(xs, ys, tile_of, offsets, owner_map, patterns, tile, probe, hi, lo):
+    tiles = xs * ys
+    piece = SIDE // tiles
+    reads = patterns.shape[0]
+    dma = pltpu.SemaphoreType.DMA
+    vmem, smem, hbm = (
+        pl.BlockSpec(memory_space=space) for space in (pltpu.VMEM, pltpu.SMEM, pl.ANY)
+    )
+    field = jax.ShapeDtypeStruct((MAX_READS, 2, SIDE, SIDE), F32)
+    return pl.pallas_call(
+        functools.partial(exchange_kernel, xs, ys),
+        out_shape=(
+            jax.ShapeDtypeStruct((4, 2 * SIDE * 4, HALF), F32),
+            jax.ShapeDtypeStruct((MAX_READS, SIDE, SIDE), F32),
+            field,
+            field,
+            jax.ShapeDtypeStruct((4, MAX_READS), jnp.int32),
+        ),
+        in_specs=[smem, smem, smem] + [hbm] * 5,
+        out_specs=(vmem, vmem, vmem, vmem, smem),
+        scratch_shapes=[
+            pltpu.VMEM(tile.shape, F32),
+            pltpu.VMEM(probe.shape, F32),
+            pltpu.VMEM(hi.shape, BF16),
+            pltpu.VMEM(lo.shape, BF16),
+            pltpu.VMEM((tiles, 1, HALF), jnp.int32),
+            pltpu.VMEM((32, HALF), jnp.int32),
+            pltpu.SMEM((32, HALF), jnp.int32),
+            pltpu.VMEM((tiles * reads, piece, SIDE), F32),
+            pltpu.VMEM((tiles, MAX_READS, piece, SIDE), F32),
+            dma((4,)), dma, dma, dma((tiles,)), dma((tiles,)), dma((tiles,)), dma((tiles,)),
+            dma((tiles,)), dma((tiles,)),
+        ],
+        cost_estimate=pl.CostEstimate(flops=MAX_READS * 24 * 2 * SIDE**3, bytes_accessed=14 << 20, transcendentals=0),
+        compiler_params=pltpu.CompilerParams(
+            collective_id=0, has_side_effects=True, vmem_limit_bytes=40 << 20
+        ),
+    )(tile_of, offsets, owner_map, patterns, tile, probe, hi, lo)
 
 
 def backward_kernel(
-    info, tile, probe, hi, lo, shuffle, back, far, pattern, grad, probe_grad, held, total, mixed
+    info, held, probe, hi, lo, shuffle, back, far, arrived, total, probe_grad, mixed
 ):
-    k = pl.program_id(0)
-
-    @pl.when(k == 0)
-    def _():
-        open_tile(tile, held)
-        total[...] = jnp.zeros_like(total)
-        probe_grad[...] = jnp.zeros_like(probe_grad)
-
-    @pl.when(k < info[3 * MAX_READS])
-    def _():
-        a, b = info[MAX_READS + k], info[2 * MAX_READS + k]
+    total[...] = jnp.zeros_like(total)
+    probe_grad[...] = jnp.zeros_like(probe_grad)
+
+    def one(k, carry):
+        a, b = info[1, k], info[2, k]
         for c in range(2):
-            mixed[c] = pattern[0, :, c * HALF : (c + 1) * HALF]
+            mixed[c] = arrived[k, :, c * HALF : (c + 1) * HALF]
         measured = jnp.concatenate(
             [
                 jnp.concatenate([mixed[c, pl.ds(odd, HALF, stride=2), :] for c in range(2)], axis=1)
@@ -220,10 +376,10 @@
         )
         mh, ml = parts(measured)
         measured = mm(mh, shuffle[...]) + mm(ml, shuffle[...])
-        fre, fim = far[0, 0], far[0, 1]
+        fre, fim = far[k, 0], far[k, 1]
         scale = 2.0 * (fre * fre + fim * fim - measured)
         gre, gim = from_far(scale * fre, scale * fim, hi, lo)
-        bre, bim = back[0, 0], back[0, 1]
+        bre, bim = back[k, 0], back[k, 1]
         add_patch(total.at[2], a, b, bre * gre + bim * gim)
         add_patch(total.at[3], a, b, bre * gim - bim * gre)
         ore, oim = patch(held.at[2], a, b), patch(held.at[3], a, b)
@@ -234,92 +390,22 @@
         ore, oim = patch(held.at[0], a, b), patch(held.at[1], a, b)
         probe_grad[0] += ore * gre + oim * gim
         probe_grad[1] += ore * gim - oim * gre
-
-    @pl.when(k == pl.num_programs(0) - 1)
-    def _():
-        close_tile(total, grad)
-
-
-def plane_scratch():
-    return pltpu.VMEM((4, 2 * SIDE * 4, HALF), F32)
-
-
-def whole(array):
-    ndim = array.ndim
-    return pl.BlockSpec(array.shape, lambda k, info: (0,) * ndim, pipeline_mode=pl.Buffered(1))
-
-
-def forward(info, tile, probe, hi, lo):
-    block = pl.BlockSpec((1, 2, SIDE, SIDE), lambda k, info: (k, 0, 0, 0))
-    out = jax.ShapeDtypeStruct((MAX_READS, 2, SIDE, SIDE), F32)
-    return pl.pallas_call(
-        forward_kernel,
-        out_shape=(out, out),
-        grid_spec=pltpu.PrefetchScalarGridSpec(
-            num_scalar_prefetch=1,
-            grid=(MAX_READS,),
-            in_specs=[whole(x) for x in (tile, probe, hi, lo)],
-            out_specs=(block, block),
-            scratch_shapes=[plane_scratch()],
-        ),
-        cost_estimate=pl.CostEstimate(
-            flops=MAX_READS * 24 * 2 * SIDE**3, bytes_accessed=14 << 20, transcendentals=0
-        ),
-        compiler_params=pltpu.CompilerParams(vmem_limit_bytes=48 << 20),
-    )(info, tile, probe, hi, lo)
-
-
-def backward(info, tile, probe, hi, lo, shuffle, back, far, arrived):
-    block = pl.BlockSpec((1, 2, SIDE, SIDE), lambda k, info: (k, 0, 0, 0))
-    pattern = pl.BlockSpec((1, SIDE, SIDE), lambda k, info: (info[k], 0, 0))
-    grad = jax.ShapeDtypeStruct((1,) + tile.shape, F32)
-    probe_grad = jax.ShapeDtypeStruct(probe.shape, F32)
+        return carry
+
+    lax.fori_loop(0, info[3, 0], one, 0)
+
+
+def backward(info, held, probe, hi, lo, shuffle, back, far, arrived):
+    vmem, smem = pl.BlockSpec(memory_space=pltpu.VMEM), pl.BlockSpec(memory_space=pltpu.SMEM)
     return pl.pallas_call(
         backward_kernel,
-        out_shape=(grad, probe_grad),
-        grid_spec=pltpu.PrefetchScalarGridSpec(
-            num_scalar_prefetch=1,
-            grid=(MAX_READS,),
-            in_specs=[whole(x) for x in (tile, probe, hi, lo, shuffle)] + [block, block, pattern],
-            out_specs=(whole(grad), whole(probe_grad)),
-            scratch_shapes=[plane_scratch(), plane_scratch(), pltpu.VMEM((2, SIDE, HALF), F32)],
-        ),
-        cost_estimate=pl.CostEstimate(
-            flops=MAX_READS * 26 * 2 * SIDE**3, bytes_accessed=20 << 20, transcendentals=0
-        ),
-        compiler_params=pltpu.CompilerParams(vmem_limit_bytes=48 << 20),
-    )(info, tile, probe, hi, lo, shuffle, back, far, arrived)
-
-
-def spread_kernel(which, patterns, out, held, in_sem, out_sem):
-    count = out.shape[0]
-    load = pltpu.make_async_copy(patterns, held, in_sem)
-    load.start()
-    load.wait()
-    copies = [pltpu.make_async_copy(held.at[which[j]], out.at[j], out_sem.at[j]) for j in range(count)]
-    for copy in copies:
-        copy.start()
-    for copy in copies:
-        copy.wait()
-
-
-def spread(which, patterns):
-    count = which.shape[0]
-    return pl.pallas_call(
-        spread_kernel,
-        out_shape=jax.ShapeDtypeStruct((count,) + patterns.shape[1:], F32),
-        in_specs=[pl.BlockSpec(memory_space=pltpu.SMEM), pl.BlockSpec(memory_space=pl.ANY)],
-        out_specs=pl.BlockSpec(memory_space=pl.ANY),
-        scratch_shapes=[
-            pltpu.VMEM(patterns.shape, F32),
-            pltpu.SemaphoreType.DMA,
-            pltpu.SemaphoreType.DMA((count,)),
-        ],
-    )(which, patterns)
-
-
-MESH = pl.DeviceIdType.MESH
-CORES = 2
+        out_shape=(jax.ShapeDtypeStruct(held.shape, F32), jax.ShapeDtypeStruct(probe.shape, F32)),
+        in_specs=[smem] + [vmem] * 8,
+        out_specs=(vmem, vmem),
+        scratch_shapes=[pltpu.VMEM((2, SIDE, HALF), F32)],
+        cost_estimate=pl.CostEstimate(flops=MAX_READS * 26 * 2 * SIDE**3, bytes_accessed=20 << 20, transcendentals=0),
+        compiler_params=pltpu.CompilerParams(vmem_limit_bytes=40 << 20),
+    )(info, held, probe, hi, lo, shuffle, back, far, arrived)
 
 
 def reduce_kernel(
@@ -328,20 +414,16 @@
     load_sem, core_send, core_recv, ring_send, ring_recv, probe_send, probe_recv, z_send, z_recv,
     all_send, all_recv, pair_send, pair_recv,
 ):
-    scan, tile = lax.axis_index("scan"), lax.axis_index("tile")
+    scan = lax.axis_index("scan")
     z, c = scan // CORES, scan % CORES
-    x, y = tile // ys, tile % ys
-    height = out.shape[3]
+    tile, at_xy, shifts = plane_steps(xs, ys)
+    height = own.shape[3]
     piece = piece_z.shape[1]
 
     def at_z(step):
         return {"scan": lax.rem(z + step + zs, zs) * CORES + c}
 
-    def at_xy(j):
-        return {"tile": lax.rem(x + j // ys, xs) * ys + lax.rem(y + j % ys, ys)}
-
     pair = {"scan": z * CORES + 1 - c}
-    shifts = range(1, xs * ys)
     steps = [2, 1, -1, 0]
 
     def rows_of(step, core):
@@ -352,17 +434,12 @@
     for partner in partners:
         pl.semaphore_signal(barrier, inc=1, device_id=partner, device_id_type=MESH)
     loads = [
-        pltpu.make_async_copy(grad.at[0, :, :, rows_of(step, c), :], own.at[k], load_sem.at[k])
+        pltpu.make_async_copy(grad.at[:, :, rows_of(step, c), :], own.at[k], load_sem.at[k])
         for k, step in enumerate(steps)
     ]
     for load in loads:
         load.start()
     pl.semaphore_wait(barrier, len(partners))
-
-    def remote(src, dst, send, recv, device):
-        return pltpu.make_async_remote_copy(
-            src_ref=src, dst_ref=dst, send_sem=send, recv_sem=recv, device_id=device, device_id_type=MESH
-        )
 
     started = []
 
@@ -373,7 +450,7 @@
 
     probe_pair = go(remote(probe.at[1 - c], plane_in, core_send.at[4], core_recv.at[4], pair))
     cores = [
-        go(remote(grad.at[0, :, :, rows_of(step, 1 - c), :], core_in.at[k], core_send.at[k], core_recv.at[k], pair))
+        go(remote(grad.at[:, :, rows_of(step, 1 - c), :], core_in.at[k], core_send.at[k], core_recv.at[k], pair))
         for k, step in enumerate(steps)
     ]
 
@@ -430,8 +507,14 @@
     down.wait_recv()
     up_sum.wait_recv()
     down_sum.wait_recv()
-    out[0, 0] = own[3, 0] + (direct_in[2] + direct_in[1])
-    out[0, 1] = own[3, 1] + (direct_in[0] + direct_in[3])
+    own[3, 0] = own[3, 0] + (direct_in[2] + direct_in[1])
+    own[3, 1] = own[3, 1] + (direct_in[0] + direct_in[3])
+    lines = out.shape[3]
+    for plane in range(4):
+        for k in range(4):
+            out[0, plane // 2, plane % 2, :, k * HALF : (k + 1) * HALF] = own[
+                3, plane // 2, plane % 2, pl.ds(k, lines, stride=4), :
+            ]
     last.wait_recv()
     for copy in started:
         copy.wait_send()
@@ -440,14 +523,14 @@
 def reduce_all(sizes, grad, probe):
     zs, xs, ys = sizes
     tiles = xs * ys
-    slices, comps, side, width = grad.shape[1:]
+    slices, comps, side, width = grad.shape
     height = side // (zs * CORES)
     piece = SIDE // tiles
     dma = pltpu.SemaphoreType.DMA
     return pl.pallas_call(
         functools.partial(reduce_kernel, zs, xs, ys),
         out_shape=(
-            jax.ShapeDtypeStruct((1, slices, comps, height, width), F32),
+            jax.ShapeDtypeStruct((1, slices, comps, height // 4, 4 * width), F32),
             jax.ShapeDtypeStruct(probe.shape, F32),
         ),
         in_specs=[pl.BlockSpec(memory_space=pl.ANY), pl.BlockSpec(memory_space=pltpu.VMEM)],
@@ -469,41 +552,18 @@
     )(grad, probe)
 
 
-def lookup(table, indices):
-    choices = jnp.arange(table.shape[0], dtype=jnp.int32)
-    return jnp.sum(jnp.where(indices[..., None] == choices, table, 0), axis=-1)
-
-
 def per_device(object_tiles, probe_wave, patterns, tile_of, offsets, owner_map):
     tile_count = lax.axis_size("tile")
-    pos_dev = tile_of.shape[0]
-    high, low, shuffle = tables()
-    high, low, shuffle = jnp.asarray(high), jnp.asarray(low), jnp.asarray(shuffle)
-    owners = jnp.arange(tile_count, dtype=jnp.int32)
-    reads = lookup(owner_map, tile_of)[None, :] == owners[:, None]
-    which = jnp.sum(jnp.where(reads, jnp.arange(pos_dev, dtype=jnp.int32), 0), axis=1)
-    notes = jnp.stack(
-        [jnp.any(reads, axis=1).astype(jnp.int32)]
-        + [jnp.sum(jnp.where(reads, offsets[:, axis], 0), axis=1) for axis in range(2)],
-        axis=1,
-    )
-    notes = lax.all_to_all(notes, "tile", split_axis=0, concat_axis=0, tiled=True)
-    notes, which = lax.optimization_barrier((notes, which))
-    arrived = lax.all_to_all(spread(which, patterns), "tile", split_axis=0, concat_axis=0, tiled=True)
-    present = notes[:, 0] > 0
-    rank = jnp.sum(jnp.where((owners[None, :] < owners[:, None]) & present[None, :], 1, 0), axis=1)
-    chosen = (rank[None, :] == jnp.arange(MAX_READS, dtype=jnp.int32)[:, None]) & present[None, :]
-    info = jnp.stack([owners, notes[:, 1], notes[:, 2]])
-    info = jnp.sum(jnp.where(chosen[None], info[:, None, :], 0), axis=2).reshape(-1)
-    info = jnp.concatenate([info, jnp.sum(notes[:, 0])[None]])
-    tile = object_tiles[0]
-    back, far = forward(info, tile, probe_wave, high, low)
-    tile_grad, probe_part = backward(
-        info, tile, probe_wave, high, low, shuffle, back, far, arrived
-    )
+    high, low, shuffle = (jnp.asarray(table) for table in tables())
     zs, xs = lax.axis_size("scan") // CORES, math.isqrt(tile_count)
-    object_part, probe_total = reduce_all((zs, xs, tile_count // xs), tile_grad, probe_part)
-    count = tile_count * lax.axis_size("scan") * pos_dev
+    ys = tile_count // xs
+    held, arrived, back, far, info = exchange(
+        xs, ys, tile_of, offsets, owner_map, patterns, object_tiles, probe_wave, high, low
+    )
+    tile_grad, probe_part = backward(info, held, probe_wave, high, low, shuffle, back, far, arrived)
+    tile_grad = tile_grad.reshape((2, 2) + tile_grad.shape[1:])
+    object_part, probe_total = reduce_all((zs, xs, ys), tile_grad, probe_part)
+    count = tile_count * lax.axis_size("scan") * patterns.shape[0]
     return object_part, probe_total / jnp.sqrt(jnp.ones((), F32) * count)
 
 

time: 143 us -> 121 us (0.85)
  waiting for transfers between devices: 38.4 us -> 0 us
  Pallas kernels: 76.4 us -> 109 us
  blocking collectives: 13.8 us -> 0 us
  local copies, waits for them, and re-layouts: 4.02 us -> 9.56 us
  starting transfers between devices: 4.68 us -> 0 us
  other arithmetic: 4.05 us -> 0.84 us
    all_to_all x1 -> x0, waiting for transfers between devices: 38.4 us -> none  [per_device(): lax.all_to_all(spread(which, patterns), 'tile', split_axis=0, concat_axis...]
    pallas_call x3 -> x2, Pallas kernels: 31.3 us -> 69.5 us  [the longest x1 48.6 us: exchange(): pl.pallas_call(functools.partial(exchange_kernel, xs, ys), out_shape=(jax...]
    all_to_all x1 -> x0, blocking collectives: 13.8 us -> none  [per_device(): lax.all_to_all(notes, 'tile', split_axis=0, concat_axis=0, tiled=True)]
    unnamed x11 -> x24, local copies, waits for them, and re-layouts: 3 us -> 9.56 us
    pallas_call x1, Pallas kernels: 45.1 us -> 39.4 us  [reduce_all(): pl.pallas_call(functools.partial(reduce_kernel, zs, xs, ys), out_shape=(j...]
    all_to_all x1 -> x0, starting transfers between devices: 4.68 us -> none  [per_device(): lax.all_to_all(spread(which, patterns), 'tile', split_axis=0, concat_axis...]
    reduce_sum x4 -> x0, other arithmetic: 1.71 us -> none  [the longest x1 0.85 us: lookup(): return jnp.sum(jnp.where(indices[..., None] == choices, table, 0), axis=-1)]
  transfers between devices with their start and end apart: 1 -> 0, of which waited for: 1 -> 0; matrix products, arithmetic and copies ran while one was open for 1% -> 0% of each run, Pallas kernels for 8% -> 0%
where the time goes in v3:
time: 121 us; the launch traced here: 120 us
  Pallas kernels  109 us (90%)
  local copies, waits for them, and re-layouts  9.56 us (8%)
    pallas_call x1, Pallas kernels, exchange(): pl.pallas_call(functools.partial(exchange_kernel, xs, ys), out_shape=(jax...  48.6 us
    pallas_call x1, Pallas kernels, reduce_all(): pl.pallas_call(functools.partial(reduce_kernel, zs, xs, ys), out_shape=(j...  39.4 us
    pallas_call x1, Pallas kernels, backward(): pl.pallas_call(backward_kernel, out_shape=(jax.ShapeDtypeStruct(held.shap...  21 us
    unnamed x24, local copies, waits for them, and re-layouts  9.56 us

profile of v3, /device:TPU:1, one launch (start us, length us, event | category | flops | bytes accessed | tf_op | source)
XLA Modules:
  0.0 120.0 jit_solution(7410097163027637583)
XLA Ops:
  0.6 0.8 copy.11.offsets
  1.4 0.0 copy-start
  1.4 1.2 %copy-done = f32[4,256,256]{2,1,0:T(8,128)S(1)} copy-done((f32[4,256,256]{2,1,0:T(8,128)S(1)}, f32[4,256,256]{2,1,0:T(8,128)}, u32[]{:S(2)}) %copy-start) | copy-done | bytes 1048600
  2.6 0.0 copy-start.1
  2.6 1.0 copy-done.1
  3.7 0.0 copy-start.3
  3.7 0.7 copy-done.3
  4.3 0.0 copy-start.4
  4.3 0.7 copy-done.4
  5.0 0.0 copy-start.5
  5.0 1.2 %copy-done.5 = bf16[8,256,256]{2,1,0:T(8,128)(2,1)S(1)} copy-done((bf16[8,256,256]{2,1,0:T(8,128)(2,1)S(1)}, bf16[8,256,256]{2,1,0:T(8,128)(2,1)}, u32[]{:S(2)}) %copy-start.5) | copy-done | bytes 1048600
  6.2 0.0 copy-start.7
  6.2 1.2 %copy-done.7 = bf16[8,256,256]{2,1,0:T(8,128)(2,1)S(1)} copy-done((bf16[8,256,256]{2,1,0:T(8,128)(2,1)S(1)}, bf16[8,256,256]{2,1,0:T(8,128)(2,1)}, u32[]{:S(2)}) %copy-start.7) | copy-done | bytes 1048600
  7.4 0.0 copy-start.2
  7.4 0.0 copy-start.6
  7.4 0.0 copy-start.8
  7.4 0.0 copy-start.9
  7.4 48.6 %shard_map.104 = (f32[4,2048,128]{2,1,0:T(8,128)S(1)}, f32[8,256,256]{2,1,0:T(8,128)S(1)}, f32[8,2,256,256]{3,2,1,0:T(8,128)S(1)}, f32[8,2,256,256]{3,2,1,0:T(8,128)}, s32[4,8]{1,0:T(4,128)S(1)}) custom-call(s32[4]{0:T(128)S(1)} %copy-done.3, s32[4,2]{1,0:T(4,128)S(1)} %copy.11.offsets, s32[16]{0:T(128)S(1)} %copy-done.4, f32[4,256,256]{2,1,0:T(8,128)S(1)} %copy-done, ...), custom_call_target="tpu_custom_call" | custom-call | flops 6442450944 | bytes 14680064 | tf_op jit(solution)/shard_map/pallas_call | solution.py:329
  56.0 0.0 copy-start.10
  56.0 2.0 %copy-done.10 = f32[8,2,256,256]{3,2,1,0:T(8,128)} copy-done((f32[8,2,256,256]{3,2,1,0:T(8,128)}, f32[8,2,256,256]{3,2,1,0:T(8,128)S(1)}, u32[]{:S(2)}) %copy-start.10) | copy-done | bytes 4194328
  58.0 0.0 copy-done.2
  58.0 0.0 copy-done.6
  58.0 0.0 copy-done.8
  58.0 0.0 copy-done.9
  58.0 21.0 %shard_map.105 = (f32[4,2048,128]{2,1,0:T(8,128)S(1)}, f32[2,256,256]{2,1,0:T(8,128)S(1)}) custom-call(s32[4,8]{1,0:T(4,128)S(1)} %get-tuple-element.11.info, f32[4,2048,128]{2,1,0:T(8,128)S(1)} %get-tuple-element.12.held, f32[2,256,256]{2,1,0:T(8,128)S(1)} %copy-done.2, bf16[8,256,256]{2,1,0:T(8,128)(2,1)S(1)} %copy-done.8, ...), custom_call_target="tpu_custom_call" | custom-call | flops 6979321856 | bytes 20971520 | tf_op jit(solution)/shard_map/pallas_call | solution.py:400
  79.0 39.4 %shard_map.106 = (f32[1,2,2,64,512]{4,3,2,1,0:T(8,128)S(1)}, f32[2,256,256]{2,1,0:T(8,128)S(1)}) custom-call(f32[2,2,2048,128]{3,2,1,0:T(8,128)S(1)} %bitcast.1, f32[2,256,256]{2,1,0:T(8,128)S(1)} %get-tuple-element.17.probe), custom_call_target="tpu_custom_call" | custom-call | tf_op jit(solution)/shard_map/pallas_call | solution.py:530
  118.4 0.8 broadcast_multiply_fusion
  119.2 0.8 copy.13
Async XLA Ops:
  1.4 1.2 %copy-start = (f32[4,256,256]{2,1,0:T(8,128)S(1)}, f32[4,256,256]{2,1,0:T(8,128)}, u32[]{:S(2)}) copy-start(f32[4,256,256]{2,1,0:T(8,128)} %patterns.1) | copy-start | bytes 3145732
  2.6 1.0 copy-start.1
  3.7 0.7 copy-start.3
  4.3 0.7 copy-start.4
  5.0 1.2 %copy-start.5 = (bf16[8,256,256]{2,1,0:T(8,128)(2,1)S(1)}, bf16[8,256,256]{2,1,0:T(8,128)(2,1)}, u32[]{:S(2)}) copy-start(bf16[8,256,256]{2,1,0:T(8,128)(2,1)} %constant.10.clone.lo_hbm.lo) | copy-start | bytes 3145732
  6.2 1.2 %copy-start.7 = (bf16[8,256,256]{2,1,0:T(8,128)(2,1)S(1)}, bf16[8,256,256]{2,1,0:T(8,128)(2,1)}, u32[]{:S(2)}) copy-start(bf16[8,256,256]{2,1,0:T(8,128)(2,1)} %constant.9.clone.hi_hbm.hi) | copy-start | bytes 3145732
  7.4 50.6 %copy-start.2 = (f32[2,256,256]{2,1,0:T(8,128)S(1)}, f32[2,256,256]{2,1,0:T(8,128)}, u32[]{:S(2)}) copy-start(f32[2,256,256]{2,1,0:T(8,128)} %probe.1) | copy-start | bytes 1572868
  7.4 50.6 %copy-start.6 = (bf16[8,256,256]{2,1,0:T(8,128)(2,1)S(1)}, bf16[8,256,256]{2,1,0:T(8,128)(2,1)}, u32[]{:S(2)}) copy-start(bf16[8,256,256]{2,1,0:T(8,128)(2,1)} %constant.10.clone.lo_hbm.lo) | copy-start | bytes 3145732
  7.4 50.6 %copy-start.8 = (bf16[8,256,256]{2,1,0:T(8,128)(2,1)S(1)}, bf16[8,256,256]{2,1,0:T(8,128)(2,1)}, u32[]{:S(2)}) copy-start(bf16[8,256,256]{2,1,0:T(8,128)(2,1)} %constant.9.clone.hi_hbm.hi) | copy-start | bytes 3145732
  7.4 50.6 %copy-start.9 = (bf16[256,256]{1,0:T(8,128)(2,1)S(1)}, bf16[256,256]{1,0:T(8,128)(2,1)}, u32[]{:S(2)}) copy-start(bf16[256,256]{1,0:T(8,128)(2,1)} %constant.11.clone.shuffle) | copy-start | bytes 393220
  56.0 2.0 %copy-start.10 = (f32[8,2,256,256]{3,2,1,0:T(8,128)}, f32[8,2,256,256]{3,2,1,0:T(8,128)S(1)}, u32[]{:S(2)}) copy-start(f32[8,2,256,256]{3,2,1,0:T(8,128)S(1)} %get-tuple-element.13.back) | copy-start | bytes 12582916

commit v4 on v3

--- a/solution.py
+++ b/solution.py
@@ -225,10 +225,10 @@
 
 
 def exchange_kernel(
-    xs, ys, tile_of, offsets, owner_map, patterns, tile, probe_hbm, hi_hbm, lo_hbm,
+    xs, ys, tile_hbm, offset_hbm, owner_hbm, patterns, tile, probe_hbm, hi_hbm, lo_hbm,
     held, arrived, back, far, info,
-    opened, probe, hi, lo, notes, lists, lists_smem, mid, stage,
-    load_sem, own_sem, list_sem, note_send, note_recv, first_send, first_recv, second_send, second_recv,
+    tile_of, offsets, owner_map, opened, probe, hi, lo, notes, lists, lists_smem, mid, stage,
+    small_sem, load_sem, own_sem, list_sem, note_send, note_recv, first_send, first_recv, second_send, second_recv,
 ):
     me, at_xy, shifts = plane_steps(xs, ys)
     piece = mid.shape[1]
@@ -240,6 +240,12 @@
     barrier = pltpu.get_barrier_semaphore()
     for j in shifts:
         pl.semaphore_signal(barrier, inc=1, device_id=at_xy(j), device_id_type=MESH)
+    smalls = [
+        pltpu.make_async_copy(src, dst, small_sem.at[k])
+        for k, (src, dst) in enumerate([(tile_hbm, tile_of), (offset_hbm, offsets), (owner_hbm, owner_map)])
+    ]
+    for load in smalls:
+        load.start()
     loads = [
         pltpu.make_async_copy(src, dst, load_sem.at[k])
         for k, (src, dst) in enumerate(
@@ -252,10 +258,12 @@
         patterns.at[:, piece_rows(me), :], mid.at[pl.ds(reads * me, reads)], own_sem
     )
     own.start()
+    for load in smalls:
+        load.wait()
     lane = lax.broadcasted_iota(jnp.int32, (1, HALF), 1)
     note = jnp.zeros((1, HALF), jnp.int32)
     for i in range(reads):
-        for f, value in enumerate((owner_map[tile_of[i]], offsets[i, 0], offsets[i, 1])):
+        for f, value in enumerate((owner_map[tile_of[i]], offsets[0, i], offsets[1, i])):
             note = jnp.where(lane == 4 * f + i, value, note)
     notes[me] = note
     pl.semaphore_wait(barrier, len(shifts))
@@ -323,7 +331,7 @@
     reads = patterns.shape[0]
     dma = pltpu.SemaphoreType.DMA
     vmem, smem, hbm = (
-        pl.BlockSpec(memory_space=space) for space in (pltpu.VMEM, pltpu.SMEM, pl.ANY)
+        pl.BlockSpec(memory_space=space) for space in (pltpu.VMEM, pltpu.SMEM, pltpu.HBM)
     )
     field = jax.ShapeDtypeStruct((MAX_READS, 2, SIDE, SIDE), F32)
     return pl.pallas_call(
@@ -335,9 +343,12 @@
             field,
             jax.ShapeDtypeStruct((4, MAX_READS), jnp.int32),
         ),
-        in_specs=[smem, smem, smem] + [hbm] * 5,
+        in_specs=[hbm] * 8,
         out_specs=(vmem, vmem, vmem, vmem, smem),
         scratch_shapes=[
+            pltpu.SMEM(tile_of.shape, jnp.int32),
+            pltpu.SMEM(offsets.shape, jnp.int32),
+            pltpu.SMEM(owner_map.shape, jnp.int32),
             pltpu.VMEM(tile.shape, F32),
             pltpu.VMEM(probe.shape, F32),
             pltpu.VMEM(hi.shape, BF16),
@@ -347,14 +358,14 @@
             pltpu.SMEM((32, HALF), jnp.int32),
             pltpu.VMEM((tiles * reads, piece, SIDE), F32),
             pltpu.VMEM((tiles, MAX_READS, piece, SIDE), F32),
-            dma((4,)), dma, dma, dma((tiles,)), dma((tiles,)), dma((tiles,)), dma((tiles,)),
+            dma((3,)), dma((4,)), dma, dma, dma((tiles,)), dma((tiles,)), dma((tiles,)), dma((tiles,)),
             dma((tiles,)), dma((tiles,)),
         ],
         cost_estimate=pl.CostEstimate(flops=MAX_READS * 24 * 2 * SIDE**3, bytes_accessed=14 << 20, transcendentals=0),
         compiler_params=pltpu.CompilerParams(
-            collective_id=0, has_side_effects=True, vmem_limit_bytes=40 << 20
+            collective_id=0, has_side_effects=True, vmem_limit_bytes=16 << 20
         ),
-    )(tile_of, offsets, owner_map, patterns, tile, probe, hi, lo)
+    )(*(pltpu.with_memory_space_constraint(x, pltpu.HBM) for x in (tile_of, offsets, owner_map, patterns, tile, probe, hi, lo)))
 
 
 def backward_kernel(
@@ -404,7 +415,7 @@
         out_specs=(vmem, vmem),
         scratch_shapes=[pltpu.VMEM((2, SIDE, HALF), F32)],
         cost_estimate=pl.CostEstimate(flops=MAX_READS * 26 * 2 * SIDE**3, bytes_accessed=20 << 20, transcendentals=0),
-        compiler_params=pltpu.CompilerParams(vmem_limit_bytes=40 << 20),
+        compiler_params=pltpu.CompilerParams(vmem_limit_bytes=8 << 20),
     )(info, held, probe, hi, lo, shuffle, back, far, arrived)
 
 
@@ -547,7 +558,7 @@
             dma((4,)), dma((4,)), dma((tiles,)), dma((tiles,)), dma, dma,
         ],
         compiler_params=pltpu.CompilerParams(
-            collective_id=1, has_side_effects=True, vmem_limit_bytes=32 << 20
+            collective_id=1, has_side_effects=True, vmem_limit_bytes=12 << 20
         ),
     )(grad, probe)
 
@@ -558,7 +569,7 @@
     zs, xs = lax.axis_size("scan") // CORES, math.isqrt(tile_count)
     ys = tile_count // xs
     held, arrived, back, far, info = exchange(
-        xs, ys, tile_of, offsets, owner_map, patterns, object_tiles, probe_wave, high, low
+        xs, ys, tile_of, offsets.T, owner_map, patterns, object_tiles, probe_wave, high, low
     )
     tile_grad, probe_part = backward(info, held, probe_wave, high, low, shuffle, back, far, arrived)
     tile_grad = tile_grad.reshape((2, 2) + tile_grad.shape[1:])

time: 121 us -> 108 us (0.89)
  local copies, waits for them, and re-layouts: 9.56 us -> 0.82 us
  Pallas kernels: 109 us -> 105 us
    pallas_call x1, Pallas kernels: 21 us -> 7.48 us  [backward(): pl.pallas_call(backward_kernel, out_shape=(jax.ShapeDtypeStruct(held.shap...]
    pallas_call x1, Pallas kernels: 39.4 us -> 50.2 us  [reduce_all(): pl.pallas_call(functools.partial(reduce_kernel, zs, xs, ys), out_shape=(j...]
    unnamed x24 -> x9, local copies, waits for them, and re-layouts: 9.56 us -> 0.82 us
    pallas_call x1, Pallas kernels: 48.6 us -> 47 us  [exchange(): pl.pallas_call(functools.partial(exchange_kernel, xs, ys), out_shape=(jax...]
where the time goes in v4:
time: 108 us; the launch traced here: 107 us
  Pallas kernels  105 us (97%)
    pallas_call x1, Pallas kernels, reduce_all(): pl.pallas_call(functools.partial(reduce_kernel, zs, xs, ys), out_shape=(j...  50.2 us
    pallas_call x1, Pallas kernels, exchange(): pl.pallas_call(functools.partial(exchange_kernel, xs, ys), out_shape=(jax...  47 us
    pallas_call x1, Pallas kernels, backward(): pl.pallas_call(backward_kernel, out_shape=(jax.ShapeDtypeStruct(held.shap...  7.48 us

profile of v4, /device:TPU:1, one launch (start us, length us, event | category | flops | bytes accessed | tf_op | source)
XLA Modules:
  0.0 107.1 jit_solution(4008526636730420256)
XLA Ops:
  0.6 0.0 copy-start
  0.6 0.0 copy-start.1
  0.7 0.0 copy-start.2
  0.7 0.0 copy-start.3
  0.7 47.0 %shard_map.104 = (f32[4,2048,128]{2,1,0:T(8,128)S(1)}, f32[8,256,256]{2,1,0:T(8,128)S(1)}, f32[8,2,256,256]{3,2,1,0:T(8,128)S(1)}, f32[8,2,256,256]{3,2,1,0:T(8,128)S(1)}, s32[4,8]{1,0:T(4,128)S(1)}) custom-call(s32[4]{0:T(128)} %tile_hbm.1, s32[2,4]{1,0:T(2,128)} %bitcast.3, s32[16]{0:T(128)} %owner_hbm.1, f32[4,256,256]{2,1,0:T(8,128)} %patterns.1, ...), custom_call_target="tpu_custom_call" | custom-call | flops 6442450944 | bytes 14680064 | tf_op jit(solution)/shard_map/pallas_call | solution.py:337
  47.7 0.0 copy-done
  47.7 0.0 copy-done.1
  47.7 0.0 copy-done.2
  47.7 0.0 copy-done.3
  47.7 7.5 %shard_map.105 = (f32[4,2048,128]{2,1,0:T(8,128)S(1)}, f32[2,256,256]{2,1,0:T(8,128)S(1)}) custom-call(s32[4,8]{1,0:T(4,128)S(1)} %get-tuple-element.11.info, f32[4,2048,128]{2,1,0:T(8,128)S(1)} %get-tuple-element.12.held, f32[2,256,256]{2,1,0:T(8,128)S(1)} %copy-done, bf16[8,256,256]{2,1,0:T(8,128)(2,1)S(1)} %copy-done.2, ...), custom_call_target="tpu_custom_call" | custom-call | flops 6979321856 | bytes 20971520 | tf_op jit(solution)/shard_map/pallas_call | solution.py:411
  55.2 50.2 %shard_map.106 = (f32[1,2,2,64,512]{4,3,2,1,0:T(8,128)S(1)}, f32[2,256,256]{2,1,0:T(8,128)S(1)}) custom-call(f32[2,2,2048,128]{3,2,1,0:T(8,128)S(1)} %bitcast.2, f32[2,256,256]{2,1,0:T(8,128)S(1)} %get-tuple-element.17.probe), custom_call_target="tpu_custom_call" | custom-call | tf_op jit(solution)/shard_map/pallas_call | solution.py:541
  105.5 0.8 broadcast_multiply_fusion
  106.3 0.8 copy.12
Async XLA Ops:
  0.6 47.1 %copy-start = (f32[2,256,256]{2,1,0:T(8,128)S(1)}, f32[2,256,256]{2,1,0:T(8,128)}, u32[]{:S(2)}) copy-start(f32[2,256,256]{2,1,0:T(8,128)} %probe.1) | copy-start | bytes 1572868
  0.6 47.1 %copy-start.1 = (bf16[8,256,256]{2,1,0:T(8,128)(2,1)S(1)}, bf16[8,256,256]{2,1,0:T(8,128)(2,1)}, u32[]{:S(2)}) copy-start(bf16[8,256,256]{2,1,0:T(8,128)(2,1)} %constant.10.clone.lo_hbm.lo) | copy-start | bytes 3145732
  0.7 47.1 %copy-start.2 = (bf16[8,256,256]{2,1,0:T(8,128)(2,1)S(1)}, bf16[8,256,256]{2,1,0:T(8,128)(2,1)}, u32[]{:S(2)}) copy-start(bf16[8,256,256]{2,1,0:T(8,128)(2,1)} %constant.9.clone.hi_hbm.hi) | copy-start | bytes 3145732
  0.7 47.1 %copy-start.3 = (bf16[256,256]{1,0:T(8,128)(2,1)S(1)}, bf16[256,256]{1,0:T(8,128)(2,1)}, u32[]{:S(2)}) copy-start(bf16[256,256]{1,0:T(8,128)(2,1)} %constant.11.clone.shuffle) | copy-start | bytes 393220

commit v5 on v4

--- a/solution.py
+++ b/solution.py
@@ -422,7 +422,7 @@
 def reduce_kernel(
     zs, xs, ys, grad, probe, out, probe_out,
     own, core_in, half_in, direct_in, plane_in, piece_in, piece_z,
-    load_sem, core_send, core_recv, ring_send, ring_recv, probe_send, probe_recv, z_send, z_recv,
+    load_sem, core_send, core_recv, ring_send, ring_recv, part_send, part_recv, probe_send, probe_recv, z_send, z_recv,
     all_send, all_recv, pair_send, pair_recv,
 ):
     scan = lax.axis_index("scan")
@@ -459,17 +459,29 @@
         started.append(copy)
         return copy
 
+    def core_copy(k):
+        rows = rows_of(steps[k], 1 - c)
+        return go(remote(grad.at[:, :, rows, :], core_in.at[k], core_send.at[k], core_recv.at[k], pair))
+
+    def piece_rows(device):
+        return pl.ds(pl.multiple_of(device["tile"] * piece, piece), piece)
+
+    cores = [core_copy(0)]
     probe_pair = go(remote(probe.at[1 - c], plane_in, core_send.at[4], core_recv.at[4], pair))
-    cores = [
-        go(remote(grad.at[:, :, rows_of(step, 1 - c), :], core_in.at[k], core_send.at[k], core_recv.at[k], pair))
-        for k, step in enumerate(steps)
-    ]
+    cores += [core_copy(k) for k in (1, 2, 3)]
 
     def merge(k):
         loads[k].wait()
         cores[k].wait_recv()
         own[k] = own[k] + core_in[k]
 
+    def direct(part):
+        half = pl.ds(part * (height // 2), height // 2)
+        return [
+            go(remote(own.at[1, 1, :, half], direct_in.at[0, :, half], part_send.at[0, part], part_recv.at[0, part], at_z(1))),
+            go(remote(own.at[2, 0, :, half], direct_in.at[1, :, half], part_send.at[1, part], part_recv.at[1, part], at_z(-1))),
+        ]
+
     merge(0)
     halves = [
         go(remote(own.at[0, 0], half_in.at[0], ring_send.at[0], ring_recv.at[0], at_z(1))),
@@ -477,32 +489,27 @@
     ]
     probe_pair.wait_recv()
     plane_in[...] = plane_in[...] + probe[c]
-
-    def piece_rows(device):
-        return pl.ds(pl.multiple_of(device["tile"] * piece, piece), piece)
-
     gathers = [
         go(remote(plane_in.at[piece_rows(at_xy(j))], piece_in.at[j], probe_send.at[j], probe_recv.at[j], at_xy(j)))
         for j in shifts
     ]
     merge(1)
-    up = go(remote(own.at[1, 1], direct_in.at[0], ring_send.at[2], ring_recv.at[2], at_z(1)))
     merge(2)
-    down = go(remote(own.at[2, 0], direct_in.at[1], ring_send.at[3], ring_recv.at[3], at_z(-1)))
+    straight = direct(0)
+    merge(3)
+    total = plane_in[piece_rows({"tile": tile}), :]
+    for copy, j in zip(gathers, shifts):
+        copy.wait_recv()
+        total = total + piece_in[j]
+    piece_z[0] = total
+    across = [go(remote(piece_z.at[0], piece_z.at[k], z_send.at[k], z_recv.at[k], at_z(k))) for k in (1, 2, 3)]
+    straight += direct(1)
     halves[0].wait_recv()
     own[1, 0] = own[1, 0] + half_in[0]
     up_sum = go(remote(own.at[1, 0], direct_in.at[2], ring_send.at[4], ring_recv.at[4], at_z(1)))
     halves[1].wait_recv()
     own[2, 1] = own[2, 1] + half_in[1]
     down_sum = go(remote(own.at[2, 1], direct_in.at[3], ring_send.at[5], ring_recv.at[5], at_z(-1)))
-
-    total = plane_in[piece_rows({"tile": tile}), :]
-    for copy, j in zip(gathers, shifts):
-        copy.wait_recv()
-        total = total + piece_in[j]
-    piece_z[0] = total
-    across = [go(remote(piece_z.at[0], piece_z.at[k], z_send.at[k], z_recv.at[k], at_z(k))) for k in (1, 2, 3)]
-    merge(3)
     for copy in across:
         copy.wait_recv()
     mine = piece_rows({"tile": tile})
@@ -514,8 +521,8 @@
     for copy in spreads:
         copy.wait_recv()
     last = go(remote(probe_out.at[c], probe_out.at[c], pair_send, pair_recv, pair))
-    up.wait_recv()
-    down.wait_recv()
+    for copy in straight:
+        copy.wait_recv()
     up_sum.wait_recv()
     down_sum.wait_recv()
     own[3, 0] = own[3, 0] + (direct_in[2] + direct_in[1])
@@ -554,7 +561,7 @@
             pltpu.VMEM((SIDE, SIDE), F32),
             pltpu.VMEM((tiles, piece, SIDE), F32),
             pltpu.VMEM((4, piece, SIDE), F32),
-            dma((4,)), dma((5,)), dma((5,)), dma((6,)), dma((6,)), dma((tiles,)), dma((tiles,)),
+            dma((4,)), dma((5,)), dma((5,)), dma((6,)), dma((6,)), dma((2, 2)), dma((2, 2)), dma((tiles,)), dma((tiles,)),
             dma((4,)), dma((4,)), dma((tiles,)), dma((tiles,)), dma, dma,
         ],
         compiler_params=pltpu.CompilerParams(

time: 108 us -> 101 us (0.935)
  Pallas kernels: 105 us -> 98.3 us
    pallas_call x1, Pallas kernels: 50.2 us -> 32.8 us  [reduce_all(): pl.pallas_call(functools.partial(reduce_kernel, zs, xs, ys), out_shape=(j...]
    pallas_call x1, Pallas kernels: 7.48 us -> 18.5 us  [backward(): pl.pallas_call(backward_kernel, out_shape=(jax.ShapeDtypeStruct(held.shap...]
where the time goes in v5:
time: 101 us
  Pallas kernels  98.3 us (97%)
    pallas_call x1, Pallas kernels, exchange(): pl.pallas_call(functools.partial(exchange_kernel, xs, ys), out_shape=(jax...  47 us
    pallas_call x1, Pallas kernels, reduce_all(): pl.pallas_call(functools.partial(reduce_kernel, zs, xs, ys), out_shape=(j...  32.8 us
    pallas_call x1, Pallas kernels, backward(): pl.pallas_call(backward_kernel, out_shape=(jax.ShapeDtypeStruct(held.shap...  18.5 us

profile of v5, /device:TPU:1, one launch (start us, length us, event | category | flops | bytes accessed | tf_op | source)
XLA Modules:
  0.0 100.7 jit_solution(3956812843982801369)
XLA Ops:
  0.6 0.0 copy-start
  0.6 0.0 copy-start.1
  0.7 0.0 copy-start.2
  0.7 0.0 copy-start.3
  0.7 47.0 %shard_map.104 = (f32[4,2048,128]{2,1,0:T(8,128)S(1)}, f32[8,256,256]{2,1,0:T(8,128)S(1)}, f32[8,2,256,256]{3,2,1,0:T(8,128)S(1)}, f32[8,2,256,256]{3,2,1,0:T(8,128)S(1)}, s32[4,8]{1,0:T(4,128)S(1)}) custom-call(s32[4]{0:T(128)} %tile_hbm.1, s32[2,4]{1,0:T(2,128)} %bitcast.3, s32[16]{0:T(128)} %owner_hbm.1, f32[4,256,256]{2,1,0:T(8,128)} %patterns.1, ...), custom_call_target="tpu_custom_call" | custom-call | flops 6442450944 | bytes 14680064 | tf_op jit(solution)/shard_map/pallas_call | solution.py:337
  47.7 0.0 copy-done
  47.7 0.0 copy-done.1
  47.7 0.0 copy-done.2
  47.7 0.0 copy-done.3
  47.7 18.5 %shard_map.105 = (f32[4,2048,128]{2,1,0:T(8,128)S(1)}, f32[2,256,256]{2,1,0:T(8,128)S(1)}) custom-call(s32[4,8]{1,0:T(4,128)S(1)} %get-tuple-element.11.info, f32[4,2048,128]{2,1,0:T(8,128)S(1)} %get-tuple-element.12.held, f32[2,256,256]{2,1,0:T(8,128)S(1)} %copy-done, bf16[8,256,256]{2,1,0:T(8,128)(2,1)S(1)} %copy-done.2, ...), custom_call_target="tpu_custom_call" | custom-call | flops 6979321856 | bytes 20971520 | tf_op jit(solution)/shard_map/pallas_call | solution.py:411
  66.3 32.8 %shard_map.106 = (f32[1,2,2,64,512]{4,3,2,1,0:T(8,128)S(1)}, f32[2,256,256]{2,1,0:T(8,128)S(1)}) custom-call(f32[2,2,2048,128]{3,2,1,0:T(8,128)S(1)} %bitcast.2, f32[2,256,256]{2,1,0:T(8,128)S(1)} %get-tuple-element.17.probe), custom_call_target="tpu_custom_call" | custom-call | tf_op jit(solution)/shard_map/pallas_call | solution.py:548
  99.1 0.8 broadcast_multiply_fusion
  99.9 0.8 copy.12
Async XLA Ops:
  0.6 47.1 %copy-start = (f32[2,256,256]{2,1,0:T(8,128)S(1)}, f32[2,256,256]{2,1,0:T(8,128)}, u32[]{:S(2)}) copy-start(f32[2,256,256]{2,1,0:T(8,128)} %probe.1) | copy-start | bytes 1572868
  0.6 47.1 %copy-start.1 = (bf16[8,256,256]{2,1,0:T(8,128)(2,1)S(1)}, bf16[8,256,256]{2,1,0:T(8,128)(2,1)}, u32[]{:S(2)}) copy-start(bf16[8,256,256]{2,1,0:T(8,128)(2,1)} %constant.10.clone.lo_hbm.lo) | copy-start | bytes 3145732
  0.7 47.1 %copy-start.2 = (bf16[8,256,256]{2,1,0:T(8,128)(2,1)S(1)}, bf16[8,256,256]{2,1,0:T(8,128)(2,1)}, u32[]{:S(2)}) copy-start(bf16[8,256,256]{2,1,0:T(8,128)(2,1)} %constant.9.clone.hi_hbm.hi) | copy-start | bytes 3145732
  0.7 47.1 %copy-start.3 = (bf16[256,256]{1,0:T(8,128)(2,1)S(1)}, bf16[256,256]{1,0:T(8,128)(2,1)}, u32[]{:S(2)}) copy-start(bf16[256,256]{1,0:T(8,128)(2,1)} %constant.11.clone.shuffle) | copy-start | bytes 393220

commit v6 on v5

--- a/solution.py
+++ b/solution.py
@@ -178,8 +178,35 @@
     return back, to_far(re * ore - im * oim, re * oim + im * ore, hi, lo)
 
 
+def backward_one(k, a, b, valid, held, probe, hi, lo, shuffle, back, far, arrived, mixed):
+    for c in range(2):
+        mixed[c] = arrived[k, :, c * HALF : (c + 1) * HALF]
+    measured = jnp.concatenate(
+        [
+            jnp.concatenate([mixed[c, pl.ds(odd, HALF, stride=2), :] for c in range(2)], axis=1)
+            for odd in range(2)
+        ],
+        axis=0,
+    )
+    mh, ml = parts(measured)
+    measured = mm(mh, shuffle[...]) + mm(ml, shuffle[...])
+    fre, fim = far[k, 0], far[k, 1]
+    scale = valid * (fre * fre + fim * fim - measured)
+    gre, gim = from_far(scale * fre, scale * fim, hi, lo)
+    bre, bim = back[k, 0], back[k, 1]
+    second = (bre * gre + bim * gim, bre * gim - bim * gre)
+    ore, oim = patch(held.at[2], a, b), patch(held.at[3], a, b)
+    gre, gim = travel(ore * gre + oim * gim, ore * gim - oim * gre, hi, lo, True)
+    pre, pim = probe[0], probe[1]
+    first = (pre * gre + pim * gim, pre * gim - pim * gre)
+    ore, oim = patch(held.at[0], a, b), patch(held.at[1], a, b)
+    return second, first, (ore * gre + oim * gim, ore * gim - oim * gre)
+
+
 MESH = pl.DeviceIdType.MESH
 CORES = 2
+EARLY = 6
+PAIR = 2
 
 
 def remote(src, dst, send, recv, device):
@@ -225,9 +252,9 @@
 
 
 def exchange_kernel(
-    xs, ys, tile_hbm, offset_hbm, owner_hbm, patterns, tile, probe_hbm, hi_hbm, lo_hbm,
-    held, arrived, back, far, info,
-    tile_of, offsets, owner_map, opened, probe, hi, lo, notes, lists, lists_smem, mid, stage,
+    xs, ys, tile_hbm, offset_hbm, owner_hbm, patterns, tile, probe_hbm, hi_hbm, lo_hbm, shuffle_hbm,
+    held, arrived, back, far, grads, probe_grad, info,
+    tile_of, offsets, owner_map, opened, probe, hi, lo, shuffle, notes, lists, lists_smem, mid, stage, mixed,
     small_sem, load_sem, own_sem, list_sem, note_send, note_recv, first_send, first_recv, second_send, second_recv,
 ):
     me, at_xy, shifts = plane_steps(xs, ys)
@@ -249,7 +276,7 @@
     loads = [
         pltpu.make_async_copy(src, dst, load_sem.at[k])
         for k, (src, dst) in enumerate(
-            [(tile, opened), (probe_hbm, probe), (hi_hbm, hi), (lo_hbm, lo)]
+            [(tile, opened), (probe_hbm, probe), (hi_hbm, hi), (lo_hbm, lo), (shuffle_hbm, shuffle)]
         )
     ]
     for load in loads:
@@ -294,38 +321,68 @@
             info[row, k] = lists_smem[MAX_READS * row + k, me]
     for k in range(MAX_READS):
         info[3, k] = lists_smem[24, me]
-    own.wait()
-    for copy in firsts:
-        copy.wait_recv()
-    seconds = []
-    for j in shifts:
-        to = at_xy(j)["tile"]
-        for k in range(MAX_READS):
-            stage[j, k] = mid[lists_smem[k, to]]
-        copy = remote(
-            stage.at[j], arrived.at[:, piece_rows(me), :], second_send.at[j], second_recv.at[j], at_xy(j)
-        )
-        copy.start()
-        seconds.append(copy)
-    for k in range(MAX_READS):
-        arrived[k, piece_rows(me), :] = mid[lists_smem[k, me]]
     for load in loads[1:]:
         load.wait()
 
-    def one(k, carry):
+    def run_forward(k, carry):
         a, b = lists_smem[MAX_READS + k, me], lists_smem[2 * MAX_READS + k, me]
         (bre, bim), (fre, fim) = forward_one(a, b, held, probe, hi, lo)
         back[k, 0], back[k, 1], far[k, 0], far[k, 1] = bre, bim, fre, fim
         return carry
 
-    lax.fori_loop(0, MAX_READS, one, 0)
-    for copy in seconds:
+    lax.fori_loop(0, MAX_READS // 2, run_forward, 0)
+    own.wait()
+    for copy in firsts:
         copy.wait_recv()
-    for copy in tells + firsts + seconds:
+
+    def second(pair, j):
+        ranks = pl.ds(PAIR * pair, PAIR)
+        return remote(
+            stage.at[j, ranks], arrived.at[ranks, piece_rows(me), :],
+            second_send.at[pair, j], second_recv.at[pair, j], at_xy(j),
+        )
+
+    for pair in range(MAX_READS // PAIR):
+        for j in shifts:
+            to = at_xy(j)["tile"]
+            for k in range(PAIR * pair, PAIR * pair + PAIR):
+                stage[j, k] = mid[lists_smem[k, to]]
+            second(pair, j).start()
+    for k in range(MAX_READS):
+        arrived[k, piece_rows(me), :] = mid[lists_smem[k, me]]
+    lax.fori_loop(MAX_READS // 2, MAX_READS, run_forward, 0)
+    probe_grad[...] = jnp.zeros_like(probe_grad)
+
+    def run_backward(k, carry):
+        a, b = lists_smem[MAX_READS + k, me], lists_smem[2 * MAX_READS + k, me]
+        valid = jnp.where(k < lists_smem[24, me], 2.0, 0.0)
+        slice1, slice0, probe_term = backward_one(
+            k, a, b, valid, held, probe, hi, lo, shuffle, back, far, arrived, mixed
+        )
+        grads[k, 0], grads[k, 1] = slice0
+        grads[k, 2], grads[k, 3] = slice1
+        probe_grad[0] += probe_term[0]
+        probe_grad[1] += probe_term[1]
+        return carry
+
+    def run_pair(pair, carry):
+        for j in shifts:
+            second(pair, j).wait_recv()
+        return lax.fori_loop(PAIR * pair, PAIR * pair + PAIR, run_backward, carry)
+
+    lax.fori_loop(0, EARLY // PAIR, run_pair, 0)
+    for pair in range(EARLY // PAIR, MAX_READS // PAIR):
+        for j in shifts:
+            second(pair, j).wait_recv()
+    for copy in tells + firsts:
         copy.wait_send()
-
-
-def exchange(xs, ys, tile_of, offsets, owner_map, patterns, tile, probe, hi, lo):
+    for pair in range(MAX_READS // PAIR):
+        for j in shifts:
+            second(pair, j).wait_send()
+
+
+def exchange(xs, ys, *operands):
+    tile_of, offsets, owner_map, patterns, tile, probe, hi, lo, shuffle = operands
     tiles = xs * ys
     piece = SIDE // tiles
     reads = patterns.shape[0]
@@ -341,10 +398,12 @@
             jax.ShapeDtypeStruct((MAX_READS, SIDE, SIDE), F32),
             field,
             field,
+            jax.ShapeDtypeStruct((EARLY, 4, SIDE, SIDE), F32),
+            jax.ShapeDtypeStruct(probe.shape, F32),
             jax.ShapeDtypeStruct((4, MAX_READS), jnp.int32),
         ),
-        in_specs=[hbm] * 8,
-        out_specs=(vmem, vmem, vmem, vmem, smem),
+        in_specs=[hbm] * 9,
+        out_specs=(vmem,) * 6 + (smem,),
         scratch_shapes=[
             pltpu.SMEM(tile_of.shape, jnp.int32),
             pltpu.SMEM(offsets.shape, jnp.int32),
@@ -353,70 +412,63 @@
             pltpu.VMEM(probe.shape, F32),
             pltpu.VMEM(hi.shape, BF16),
             pltpu.VMEM(lo.shape, BF16),
+            pltpu.VMEM(shuffle.shape, BF16),
             pltpu.VMEM((tiles, 1, HALF), jnp.int32),
             pltpu.VMEM((32, HALF), jnp.int32),
             pltpu.SMEM((32, HALF), jnp.int32),
             pltpu.VMEM((tiles * reads, piece, SIDE), F32),
             pltpu.VMEM((tiles, MAX_READS, piece, SIDE), F32),
-            dma((3,)), dma((4,)), dma, dma, dma((tiles,)), dma((tiles,)), dma((tiles,)), dma((tiles,)),
-            dma((tiles,)), dma((tiles,)),
+            pltpu.VMEM((2, SIDE, HALF), F32),
+            dma((3,)), dma((5,)), dma, dma, dma((tiles,)), dma((tiles,)), dma((tiles,)), dma((tiles,)),
+            dma((MAX_READS // PAIR, tiles)), dma((MAX_READS // PAIR, tiles)),
         ],
         cost_estimate=pl.CostEstimate(flops=MAX_READS * 24 * 2 * SIDE**3, bytes_accessed=14 << 20, transcendentals=0),
         compiler_params=pltpu.CompilerParams(
             collective_id=0, has_side_effects=True, vmem_limit_bytes=16 << 20
         ),
-    )(*(pltpu.with_memory_space_constraint(x, pltpu.HBM) for x in (tile_of, offsets, owner_map, patterns, tile, probe, hi, lo)))
+    )(*(pltpu.with_memory_space_constraint(x, pltpu.HBM) for x in operands))
 
 
 def backward_kernel(
-    info, held, probe, hi, lo, shuffle, back, far, arrived, total, probe_grad, mixed
+    info, held, probe, hi, lo, shuffle, back, far, arrived, grads, probe_early,
+    total, probe_grad, mixed,
 ):
     total[...] = jnp.zeros_like(total)
-    probe_grad[...] = jnp.zeros_like(probe_grad)
+    probe_grad[...] = probe_early[...]
+    reads = info[3, 0]
+
+    def add(k, carry):
+        a, b = info[1, k], info[2, k]
+        for plane in range(4):
+            add_patch(total.at[plane], a, b, grads[k, plane])
+        return carry
 
     def one(k, carry):
         a, b = info[1, k], info[2, k]
-        for c in range(2):
-            mixed[c] = arrived[k, :, c * HALF : (c + 1) * HALF]
-        measured = jnp.concatenate(
-            [
-                jnp.concatenate([mixed[c, pl.ds(odd, HALF, stride=2), :] for c in range(2)], axis=1)
-                for odd in range(2)
-            ],
-            axis=0,
+        slice1, slice0, probe_term = backward_one(
+            k, a, b, 2.0, held, probe, hi, lo, shuffle, back, far, arrived, mixed
         )
-        mh, ml = parts(measured)
-        measured = mm(mh, shuffle[...]) + mm(ml, shuffle[...])
-        fre, fim = far[k, 0], far[k, 1]
-        scale = 2.0 * (fre * fre + fim * fim - measured)
-        gre, gim = from_far(scale * fre, scale * fim, hi, lo)
-        bre, bim = back[k, 0], back[k, 1]
-        add_patch(total.at[2], a, b, bre * gre + bim * gim)
-        add_patch(total.at[3], a, b, bre * gim - bim * gre)
-        ore, oim = patch(held.at[2], a, b), patch(held.at[3], a, b)
-        gre, gim = travel(ore * gre + oim * gim, ore * gim - oim * gre, hi, lo, True)
-        pre, pim = probe[0], probe[1]
-        add_patch(total.at[0], a, b, pre * gre + pim * gim)
-        add_patch(total.at[1], a, b, pre * gim - pim * gre)
-        ore, oim = patch(held.at[0], a, b), patch(held.at[1], a, b)
-        probe_grad[0] += ore * gre + oim * gim
-        probe_grad[1] += ore * gim - oim * gre
+        for plane, value in enumerate(slice0 + slice1):
+            add_patch(total.at[plane], a, b, value)
+        probe_grad[0] += probe_term[0]
+        probe_grad[1] += probe_term[1]
         return carry
 
-    lax.fori_loop(0, info[3, 0], one, 0)
-
-
-def backward(info, held, probe, hi, lo, shuffle, back, far, arrived):
+    lax.fori_loop(0, jnp.minimum(reads, EARLY), add, 0)
+    lax.fori_loop(EARLY, reads, one, 0)
+
+
+def backward(info, held, probe, *operands):
     vmem, smem = pl.BlockSpec(memory_space=pltpu.VMEM), pl.BlockSpec(memory_space=pltpu.SMEM)
     return pl.pallas_call(
         backward_kernel,
         out_shape=(jax.ShapeDtypeStruct(held.shape, F32), jax.ShapeDtypeStruct(probe.shape, F32)),
-        in_specs=[smem] + [vmem] * 8,
+        in_specs=[smem] + [vmem] * (2 + len(operands)),
         out_specs=(vmem, vmem),
         scratch_shapes=[pltpu.VMEM((2, SIDE, HALF), F32)],
         cost_estimate=pl.CostEstimate(flops=MAX_READS * 26 * 2 * SIDE**3, bytes_accessed=20 << 20, transcendentals=0),
         compiler_params=pltpu.CompilerParams(vmem_limit_bytes=8 << 20),
-    )(info, held, probe, hi, lo, shuffle, back, far, arrived)
+    )(info, held, probe, *operands)
 
 
 def reduce_kernel(
@@ -575,10 +627,12 @@
     high, low, shuffle = (jnp.asarray(table) for table in tables())
     zs, xs = lax.axis_size("scan") // CORES, math.isqrt(tile_count)
     ys = tile_count // xs
-    held, arrived, back, far, info = exchange(
-        xs, ys, tile_of, offsets.T, owner_map, patterns, object_tiles, probe_wave, high, low
-    )
-    tile_grad, probe_part = backward(info, held, probe_wave, high, low, shuffle, back, far, arrived)
+    held, arrived, back, far, grads, probe_early, info = exchange(
+        xs, ys, tile_of, offsets.T, owner_map, patterns, object_tiles, probe_wave, high, low, shuffle
+    )
+    tile_grad, probe_part = backward(
+        info, held, probe_wave, high, low, shuffle, back, far, arrived, grads, probe_early
+    )
     tile_grad = tile_grad.reshape((2, 2) + tile_grad.shape[1:])
     object_part, probe_total = reduce_all((zs, xs, ys), tile_grad, probe_part)
     count = tile_count * lax.axis_size("scan") * patterns.shape[0]

time: 101 us -> 88.9 us (0.88)
  Pallas kernels: 98.3 us -> 86.4 us
    pallas_call x1, Pallas kernels: 18.5 us -> 2.07 us  [backward(): pl.pallas_call(backward_kernel, out_shape=(jax.ShapeDtypeStruct(held.shap...]
    pallas_call x1, Pallas kernels: 32.8 us -> 37.2 us  [reduce_all(): pl.pallas_call(functools.partial(reduce_kernel, zs, xs, ys), out_shape=(j...]
where the time goes in v6:
time: 88.9 us; the launch traced here: 88.8 us
  Pallas kernels  86.4 us (97%)
    pallas_call x1, Pallas kernels, exchange(): pl.pallas_call(functools.partial(exchange_kernel, xs, ys), out_shape=(jax...  47.1 us
    pallas_call x1, Pallas kernels, reduce_all(): pl.pallas_call(functools.partial(reduce_kernel, zs, xs, ys), out_shape=(j...  37.2 us
    pallas_call x1, Pallas kernels, backward(): pl.pallas_call(backward_kernel, out_shape=(jax.ShapeDtypeStruct(held.shap...  2.07 us

profile of v6, /device:TPU:1, one launch (start us, length us, event | category | flops | bytes accessed | tf_op | source)
XLA Modules:
  0.0 88.8 jit_solution(13726613291931957220)
XLA Ops:
  0.6 0.0 copy-start
  0.6 0.0 copy-start.1
  0.7 0.0 copy-start.2
  0.7 0.0 copy-start.3
  0.7 47.1 %shard_map.104 = (f32[4,2048,128]{2,1,0:T(8,128)S(1)}, f32[8,256,256]{2,1,0:T(8,128)S(1)}, f32[8,2,256,256]{3,2,1,0:T(8,128)S(1)}, f32[8,2,256,256]{3,2,1,0:T(8,...) custom-call(s32[4]{0:T(128)} %tile_hbm.1, s32[2,4]{1,0:T(2,128)} %bitcast.3, ...), custom_call_target="tpu_custom_call" | custom-call | flops 6442450944 | bytes 14680064 | tf_op jit(solution)/shard_map/pallas_call | solution.py:394
  47.8 0.0 copy-done
  47.8 0.0 copy-done.1
  47.8 0.0 copy-done.2
  47.9 0.0 copy-done.3
  47.9 2.1 %shard_map.105 = (f32[4,2048,128]{2,1,0:T(8,128)S(1)}, f32[2,256,256]{2,1,0:T(8,128)S(1)}) custom-call(s32[4,8]{1,0:T(4,128)S(1)} %get-tuple-element.13.info, f32[4,2048,128]{2,1,0:T(8,128)S(1)} %get-tuple-element.14.held, f32[2,256,256]{2,1,0:T(8,128)S(1)} %copy-done, bf16[8,256,256]{2,1,0:T(8,128)(2,1)S(1)} %copy-done.2, ...), custom_call_target="tpu_custom_call" | custom-call | flops 6979321856 | bytes 20971520 | tf_op jit(solution)/shard_map/pallas_call | solution.py:463
  49.9 37.2 %shard_map.106 = (f32[1,2,2,64,512]{4,3,2,1,0:T(8,128)S(1)}, f32[2,256,256]{2,1,0:T(8,128)S(1)}) custom-call(f32[2,2,2048,128]{3,2,1,0:T(8,128)S(1)} %bitcast.2, f32[2,256,256]{2,1,0:T(8,128)S(1)} %get-tuple-element.21.probe), custom_call_target="tpu_custom_call" | custom-call | tf_op jit(solution)/shard_map/pallas_call | solution.py:600
  87.1 0.8 broadcast_multiply_fusion
  88.0 0.8 copy.12
Async XLA Ops:
  0.6 47.2 %copy-start = (f32[2,256,256]{2,1,0:T(8,128)S(1)}, f32[2,256,256]{2,1,0:T(8,128)}, u32[]{:S(2)}) copy-start(f32[2,256,256]{2,1,0:T(8,128)} %probe.1) | copy-start | bytes 1572868
  0.6 47.2 %copy-start.1 = (bf16[8,256,256]{2,1,0:T(8,128)(2,1)S(1)}, bf16[8,256,256]{2,1,0:T(8,128)(2,1)}, u32[]{:S(2)}) copy-start(bf16[8,256,256]{2,1,0:T(8,128)(2,1)} %constant.10.clone.lo_hbm.lo) | copy-start | bytes 3145732
  0.7 47.2 %copy-start.2 = (bf16[8,256,256]{2,1,0:T(8,128)(2,1)S(1)}, bf16[8,256,256]{2,1,0:T(8,128)(2,1)}, u32[]{:S(2)}) copy-start(bf16[8,256,256]{2,1,0:T(8,128)(2,1)} %constant.9.clone.hi_hbm.hi) | copy-start | bytes 3145732
  0.7 47.2 %copy-start.3 = (bf16[256,256]{1,0:T(8,128)(2,1)S(1)}, bf16[256,256]{1,0:T(8,128)(2,1)}, u32[]{:S(2)}) copy-start(bf16[256,256]{1,0:T(8,128)(2,1)} %constant.11.clone.shuffle_hbm.shuffle) | copy-start | bytes 393220

commit v7 on v6

v7 whole, which is shorter than its diff:
```python
import functools
import math

import jax
import jax.numpy as jnp
import ml_dtypes
import numpy as np
from jax import lax
from jax.experimental import pallas as pl
from jax.experimental.pallas import tpu as pltpu
from jax.sharding import PartitionSpec as P

PROP_PHASE = 0.75
SIDE = 256
HALF = 128
MAX_READS = 8
F32 = jnp.float32
BF16 = jnp.bfloat16


def embed(block):
    return np.block([[block.real, block.imag], [-block.imag, block.real]])


@functools.cache
def tables():
    index = np.arange(SIDE)
    freq = np.where(index < HALF, index, index - SIDE).astype(np.float64)
    wave = np.exp(-2j * math.pi * (index[:, None] * index[None, :] % SIDE) / SIDE) / math.sqrt(SIDE)
    step = np.exp(-1j * PROP_PHASE * freq**2 / SIDE)
    travel = wave.conj() @ (step[:, None] * wave)
    plus = (travel[:HALF, :HALF] + travel[:HALF, HALF:]) / 2
    minus = (travel[:HALF, :HALF] - travel[:HALF, HALF:]) / 2
    forms = []
    for block in (plus, minus, wave[:HALF, 0::2], wave[:HALF, 1::2]):
        form = embed(block)
        forms += [form, form.T]
    forms = np.stack(forms)
    high = forms.astype(ml_dtypes.bfloat16)
    low = (forms - high.astype(np.float64)).astype(ml_dtypes.bfloat16)
    shuffle = np.zeros((SIDE, SIDE), ml_dtypes.bfloat16)
    shuffle[2 * np.arange(HALF), np.arange(HALF)] = 1
    shuffle[2 * np.arange(HALF) + 1, HALF + np.arange(HALF)] = 1
    return high, low, shuffle


A_PLUS, A_MINUS, F_EVEN, F_ODD = 0, 2, 4, 6


def parts(x):
    high = x.astype(BF16)
    return high, (x - high.astype(F32)).astype(BF16)


def mm(x, y):
    return jnp.dot(x, y, preferred_element_type=F32)


def right(x, high_ref, low_ref, which):
    xh, xl = parts(x)
    wh, wl = high_ref[which], low_ref[which]
    total = mm(xh, wh)
    total = total + mm(xl, wh)
    return total + mm(xh, wl)


def left(x, high_ref, low_ref, which):
    xh, xl = parts(x)
    wh, wl = high_ref[which], low_ref[which]
    total = mm(wh, xh)
    total = total + mm(wl, xh)
    return total + mm(wh, xl)


def cols(re, im):
    return (
        jnp.concatenate([re[:, :HALF] + re[:, HALF:], im[:, :HALF] + im[:, HALF:]], axis=1),
        jnp.concatenate([re[:, :HALF] - re[:, HALF:], im[:, :HALF] - im[:, HALF:]], axis=1),
    )


def rows(re, im):
    return (
        jnp.concatenate([re[:HALF] + re[HALF:], im[:HALF] + im[HALF:]], axis=0),
        jnp.concatenate([re[:HALF] - re[HALF:], im[:HALF] - im[HALF:]], axis=0),
    )


def split_cols(p, q):
    return (
        jnp.concatenate([p[:, :HALF], q[:, :HALF]], axis=1),
        jnp.concatenate([p[:, HALF:], q[:, HALF:]], axis=1),
    )


def split_rows(p, q):
    return (
        jnp.concatenate([p[:HALF], q[:HALF]], axis=0),
        jnp.concatenate([p[HALF:], q[HALF:]], axis=0),
    )


def travel(re, im, hi, lo, conj):
    flip = 1 if conj else 0
    s, d = cols(re, im)
    p, q = right(s, hi, lo, A_PLUS + flip), right(d, hi, lo, A_MINUS + flip)
    re, im = split_cols(p + q, p - q)
    s, d = rows(re, im)
    p, q = left(s, hi, lo, A_PLUS + 1 - flip), left(d, hi, lo, A_MINUS + 1 - flip)
    return split_rows(p + q, p - q)


def to_far(re, im, hi, lo):
    s, d = cols(re, im)
    re, im = split_cols(right(s, hi, lo, F_EVEN), right(d, hi, lo, F_ODD))
    s, d = rows(re, im)
    return split_rows(left(s, hi, lo, F_EVEN + 1), left(d, hi, lo, F_ODD + 1))


def from_far(re, im, hi, lo):
    even, odd = (
        jnp.concatenate([re[:, :HALF], im[:, :HALF]], axis=1),
        jnp.concatenate([re[:, HALF:], im[:, HALF:]], axis=1),
    )
    p, q = right(even, hi, lo, F_EVEN + 1), right(odd, hi, lo, F_ODD + 1)
    re, im = split_cols(p + q, p - q)
    even, odd = (
        jnp.concatenate([re[:HALF], im[:HALF]], axis=0),
        jnp.concatenate([re[HALF:], im[HALF:]], axis=0),
    )
    p, q = left(even, hi, lo, F_EVEN), left(odd, hi, lo, F_ODD)
    return split_rows(p + q, p - q)


def lane_mask(shift):
    return lax.broadcasted_iota(jnp.int32, (SIDE, HALF), 1) < shift


def patch(rows_ref, comp, a, b):
    base, shift = b // HALF, b % HALF
    back = lax.rem(HALF - shift, HALF)
    tiles = [
        pltpu.roll(
            rows_ref[pl.ds(8 * a + 4 * comp + jnp.minimum(base + k, 3), SIDE, stride=8), :], back, 1
        )
        for k in range(3)
    ]
    mask = lane_mask(HALF - shift)
    return jnp.concatenate(
        [jnp.where(mask, tiles[0], tiles[1]), jnp.where(mask, tiles[1], tiles[2])], axis=1
    )


def place(padded, comp, b, value):
    base, shift = b // HALF, b % HALF
    first, second = pltpu.roll(value[:, :HALF], shift, 1), pltpu.roll(value[:, HALF:], shift, 1)
    mask = lane_mask(shift)
    zero = jnp.zeros_like(first)
    u0, u1, u2 = (
        jnp.where(mask, zero, first), jnp.where(mask, first, second), jnp.where(mask, second, zero)
    )
    at0, below2 = lane_mask(HALF * (1 - base)), lane_mask(HALF * (2 - base))
    placed = (
        jnp.where(at0, u0, zero),
        jnp.where(at0, u1, jnp.where(below2, u0, zero)),
        jnp.where(at0, u2, jnp.where(below2, u1, u0)),
        jnp.where(at0, zero, jnp.where(below2, u2, u1)),
    )
    for c in range(4):
        padded[pl.ds(8 * SIDE + 4 * comp + c, SIDE, stride=8), :] = placed[c]


def open_tile(tile, held):
    for part in range(2):
        for comp in range(2):
            for c in range(4):
                held[part, pl.ds(4 * comp + c, 2 * SIDE, stride=8), :] = tile[
                    part, comp, :, c * HALF : (c + 1) * HALF
                ]


def forward_one(a, b, held, probe, hi, lo):
    ore, oim = patch(held.at[0], 0, a, b), patch(held.at[0], 1, a, b)
    pre, pim = probe[0], probe[1]
    back = travel(pre * ore - pim * oim, pre * oim + pim * ore, hi, lo, False)
    ore, oim = patch(held.at[1], 0, a, b), patch(held.at[1], 1, a, b)
    re, im = back
    return back, to_far(re * ore - im * oim, re * oim + im * ore, hi, lo)


def backward_one(k, a, b, valid, held, probe, hi, lo, shuffle, back, far, arrived, mixed):
    for c in range(2):
        mixed[c] = arrived[k, :, c * HALF : (c + 1) * HALF]
    measured = jnp.concatenate(
        [
            jnp.concatenate([mixed[c, pl.ds(odd, HALF, stride=2), :] for c in range(2)], axis=1)
            for odd in range(2)
        ],
        axis=0,
    )
    mh, ml = parts(measured)
    measured = mm(mh, shuffle[...]) + mm(ml, shuffle[...])
    fre, fim = far[k, 0], far[k, 1]
    scale = valid * (fre * fre + fim * fim - measured)
    gre, gim = from_far(scale * fre, scale * fim, hi, lo)
    bre, bim = back[k, 0], back[k, 1]
    second = (bre * gre + bim * gim, bre * gim - bim * gre)
    ore, oim = patch(held.at[1], 0, a, b), patch(held.at[1], 1, a, b)
    gre, gim = travel(ore * gre + oim * gim, ore * gim - oim * gre, hi, lo, True)
    pre, pim = probe[0], probe[1]
    first = (pre * gre + pim * gim, pre * gim - pim * gre)
    ore, oim = patch(held.at[0], 0, a, b), patch(held.at[0], 1, a, b)
    return second, first, (ore * gre + oim * gim, ore * gim - oim * gre)


MESH = pl.DeviceIdType.MESH
CORES = 2
AHEAD = 4


def remote(src, dst, send, recv, device):
    return pltpu.make_async_remote_copy(
        src_ref=src, dst_ref=dst, send_sem=send, recv_sem=recv, device_id=device, device_id_type=MESH
    )


def plane_steps(xs, ys):
    tile = lax.axis_index("tile")
    x, y = tile // ys, tile % ys

    def at_xy(j):
        return {"tile": lax.rem(x + j // ys, xs) * ys + lax.rem(y + j % ys, ys)}

    return tile, at_xy, range(1, xs * ys)


def read_lists(notes, tables_ref):
    count = notes.shape[0]
    note = notes[:, 0, :]
    owner = lax.broadcasted_iota(jnp.int32, note.shape, 1)
    source = lax.broadcasted_iota(jnp.int32, note.shape, 0)
    here = jnp.zeros(note.shape, jnp.int32)
    values = [jnp.zeros(note.shape, jnp.int32) for _ in range(3)]
    for i in range(4):
        hit = jnp.where(jnp.broadcast_to(note[:, i : i + 1], note.shape) == owner, 1, 0)
        here = here + hit
        fields = [4 * source + i] + [
            jnp.broadcast_to(note[:, 4 * f + i : 4 * f + i + 1], note.shape) for f in (1, 2)
        ]
        values = [v + hit * f for v, f in zip(values, fields)]
    lower = (
        lax.broadcasted_iota(jnp.int32, (count, count), 0) > lax.broadcasted_iota(jnp.int32, (count, count), 1)
    ).astype(F32)
    rank = mm(lower.astype(BF16), here.astype(F32).astype(BF16)).astype(jnp.int32)
    for k in range(MAX_READS):
        chosen = here * jnp.where(rank == k, 1, 0)
        for f in range(3):
            row = MAX_READS * f + k
            tables_ref[row : row + 1, :] = jnp.sum(chosen * values[f], axis=0, keepdims=True)
    tables_ref[24:25, :] = jnp.sum(here, axis=0, keepdims=True)


def whole_kernel(
    zs, xs, ys,
    tile_hbm, offset_hbm, owner_hbm, patterns, tile, probe_hbm, hi_hbm, lo_hbm, shuffle_hbm,
    out, probe_out,
    tile_of, offsets, owner_map, opened, probe, hi, lo, shuffle, notes, lists, lists_smem, mid, stage,
    held, arrived, back, far, mixed, padded, grad, probe_grad,
    own, core_in, half_in, direct_in, plane_in, piece_in, piece_z,
    small_sem, load_sem, own_sem, list_sem, note_send, note_recv, first_send, first_recv,
    second_send, second_recv, core_send, core_recv, ring_send, ring_recv, part_send, part_recv,
    probe_send, probe_recv, z_send, z_recv, all_send, all_recv, pair_send, pair_recv,
):
    scan = lax.axis_index("scan")
    z, c = scan // CORES, scan % CORES
    me, at_xy, shifts = plane_steps(xs, ys)
    piece = mid.shape[1]
    reads = patterns.shape[0]
    height = own.shape[2]

    def at_z(step):
        return {"scan": lax.rem(z + step + zs, zs) * CORES + c}

    pair = {"scan": z * CORES + 1 - c}

    def piece_rows(index):
        return pl.ds(pl.multiple_of(index * piece, piece), piece)

    barrier = pltpu.get_barrier_semaphore()
    partners = [pair] + [at_z(step) for step in (1, 2, 3)] + [at_xy(j) for j in shifts]
    for partner in partners:
        pl.semaphore_signal(barrier, inc=1, device_id=partner, device_id_type=MESH)
    smalls = [
        pltpu.make_async_copy(src, dst, small_sem.at[k])
        for k, (src, dst) in enumerate([(tile_hbm, tile_of), (offset_hbm, offsets), (owner_hbm, owner_map)])
    ]
    loads = [
        pltpu.make_async_copy(src, dst, load_sem.at[k])
        for k, (src, dst) in enumerate(
            [(tile, opened), (probe_hbm, probe), (hi_hbm, hi), (lo_hbm, lo), (shuffle_hbm, shuffle)]
        )
    ]
    mine = pltpu.make_async_copy(
        patterns.at[:, piece_rows(me), :], mid.at[pl.ds(reads * me, reads)], own_sem
    )
    for load in smalls + loads + [mine]:
        load.start()
    for load in smalls:
        load.wait()
    lane = lax.broadcasted_iota(jnp.int32, (1, HALF), 1)
    note = jnp.zeros((1, HALF), jnp.int32)
    for i in range(reads):
        for f, value in enumerate((owner_map[tile_of[i]], offsets[0, i], offsets[1, i])):
            note = jnp.where(lane == 4 * f + i, value, note)
    notes[me] = note
    pl.semaphore_wait(barrier, len(partners))

    tells = [
        remote(notes.at[me], notes.at[me], note_send.at[j], note_recv.at[j], at_xy(j)) for j in shifts
    ]
    firsts = [
        remote(
            patterns.at[:, piece_rows(at_xy(j)["tile"]), :], mid.at[pl.ds(reads * me, reads)],
            first_send.at[j], first_recv.at[j], at_xy(j),
        )
        for j in shifts
    ]
    for copy in tells + firsts:
        copy.start()
    loads[0].wait()
    open_tile(opened.at[0], held)
    for copy in tells:
        copy.wait_recv()
    lists[...] = jnp.zeros_like(lists)
    read_lists(notes, lists)
    listed = pltpu.make_async_copy(lists, lists_smem, list_sem)
    listed.start()
    listed.wait()
    for load in loads[1:]:
        load.wait()

    def where(k):
        return lists_smem[MAX_READS + k, me], lists_smem[2 * MAX_READS + k, me]

    def run_forward(k, carry):
        a, b = where(k)
        (bre, bim), (fre, fim) = forward_one(a, b, held, probe, hi, lo)
        back[k, 0], back[k, 1], far[k, 0], far[k, 1] = bre, bim, fre, fim
        return carry

    lax.fori_loop(0, AHEAD, run_forward, 0)
    mine.wait()
    for copy in firsts:
        copy.wait_recv()

    def second(k, j):
        return remote(
            stage.at[j, k], arrived.at[k, piece_rows(me), :],
            second_send.at[k, j], second_recv.at[k, j], at_xy(j),
        )

    def send_rank(k, carry):
        for j in shifts:
            stage[j, k] = mid[lists_smem[k, at_xy(j)["tile"]]]
            second(k, j).start()
        arrived[k, piece_rows(me), :] = mid[lists_smem[k, me]]
        return carry

    lax.fori_loop(0, MAX_READS, send_rank, 0)
    lax.fori_loop(AHEAD, MAX_READS, run_forward, 0)
    probe_grad[...] = jnp.zeros_like(probe_grad)
    grad[...] = jnp.zeros_like(grad)
    padded[...] = jnp.zeros_like(padded)

    def run_backward(k, carry):
        a, b = where(k)
        valid = jnp.where(k < lists_smem[24, me], 2.0, 0.0)
        for j in shifts:
            second(k, j).wait_recv()
        slice1, slice0, probe_term = backward_one(
            k, a, b, valid, held, probe, hi, lo, shuffle, back, far, arrived, mixed
        )
        for part, values in enumerate((slice0, slice1)):
            for comp in range(2):
                place(padded.at[part], comp, b, values[comp])
        probe_grad[0] += probe_term[0]
        probe_grad[1] += probe_term[1]
        lines = 256

        def add(i, inner):
            for part in range(2):
                to = pl.ds(pl.multiple_of(i * lines, 8), lines)
                source = pl.ds((SIDE - a + i * (lines // 8)) * 8, lines)
                grad[part, to, :] = grad[part, to, :] + padded[part, source, :]
            return inner

        lax.fori_loop(0, 8 * 2 * SIDE // lines, add, 0)
        return carry

    lax.fori_loop(0, MAX_READS, run_backward, 0)

    steps = [2, 1, -1, 0]

    def rows_of(step, core):
        return pl.ds(pl.multiple_of((lax.rem(z + step + zs, zs) * CORES + core) * height, height), height)

    started = []

    def go(copy):
        copy.start()
        started.append(copy)
        return copy

    def core_copy(k):
        return go(remote(grad.at[:, rows_of(steps[k], 1 - c), :], core_in.at[k], core_send.at[k], core_recv.at[k], pair))

    cores = [core_copy(0)]
    probe_pair = go(remote(probe_grad.at[1 - c], plane_in, core_send.at[4], core_recv.at[4], pair))
    cores += [core_copy(k) for k in (1, 2, 3)]

    def merge(k):
        cores[k].wait_recv()
        own[k] = grad[:, rows_of(steps[k], c), :] + core_in[k]

    def direct(part):
        half = pl.ds(part * (height // 2), height // 2)
        return [
            go(remote(own.at[1, 1, half], direct_in.at[0, half], part_send.at[0, part], part_recv.at[0, part], at_z(1))),
            go(remote(own.at[2, 0, half], direct_in.at[1, half], part_send.at[1, part], part_recv.at[1, part], at_z(-1))),
        ]

    merge(0)
    halves = [
        go(remote(own.at[0, 0], half_in.at[0], ring_send.at[0], ring_recv.at[0], at_z(1))),
        go(remote(own.at[0, 1], half_in.at[1], ring_send.at[1], ring_recv.at[1], at_z(-1))),
    ]
    probe_pair.wait_recv()
    plane_in[...] = plane_in[...] + probe_grad[c]
    gathers = [
        go(remote(plane_in.at[piece_rows(at_xy(j)["tile"])], piece_in.at[j], probe_send.at[j], probe_recv.at[j], at_xy(j)))
        for j in shifts
    ]
    merge(1)
    merge(2)
    straight = direct(0)
    merge(3)
    total = plane_in[piece_rows(me), :]
    for copy, j in zip(gathers, shifts):
        copy.wait_recv()
        total = total + piece_in[j]
    piece_z[0] = total
    across = [go(remote(piece_z.at[0], piece_z.at[k], z_send.at[k], z_recv.at[k], at_z(k))) for k in (1, 2, 3)]
    straight += direct(1)
    halves[0].wait_recv()
    own[1, 0] = own[1, 0] + half_in[0]
    up_sum = go(remote(own.at[1, 0], direct_in.at[2], ring_send.at[2], ring_recv.at[2], at_z(1)))
    halves[1].wait_recv()
    own[2, 1] = own[2, 1] + half_in[1]
    down_sum = go(remote(own.at[2, 1], direct_in.at[3], ring_send.at[3], ring_recv.at[3], at_z(-1)))
    for copy in across:
        copy.wait_recv()
    probe_out[c, piece_rows(me), :] = (piece_z[0] + piece_z[1]) + (piece_z[2] + piece_z[3])
    spreads = [
        go(remote(probe_out.at[c, piece_rows(me)], probe_out.at[c, piece_rows(me)], all_send.at[j], all_recv.at[j], at_xy(j)))
        for j in shifts
    ]
    for copy in spreads:
        copy.wait_recv()
    last = go(remote(probe_out.at[c], probe_out.at[c], pair_send, pair_recv, pair))
    for copy in straight:
        copy.wait_recv()
    up_sum.wait_recv()
    down_sum.wait_recv()
    own[3, 0] = own[3, 0] + (direct_in[2] + direct_in[1])
    own[3, 1] = own[3, 1] + (direct_in[0] + direct_in[3])
    lines = out.shape[3]
    for plane in range(4):
        for k in range(4):
            out[0, plane // 2, plane % 2, :, k * HALF : (k + 1) * HALF] = own[
                3, plane // 2, pl.ds(4 * (plane % 2) + k, lines, stride=8), :
            ]
    last.wait_recv()
    for copy in tells + firsts + started:
        copy.wait_send()

    def sent(k, carry):
        for j in shifts:
            second(k, j).wait_send()
        return carry

    lax.fori_loop(0, MAX_READS, sent, 0)


def whole(zs, xs, ys, *operands):
    tile_of, offsets, owner_map, patterns, tile, probe, hi, lo, shuffle = operands
    tiles = xs * ys
    piece = SIDE // tiles
    reads = patterns.shape[0]
    lines = 2 * SIDE // (zs * CORES)
    height = 8 * lines
    dma = pltpu.SemaphoreType.DMA

    def vmem(*shape):
        return pltpu.VMEM(shape, F32)

    return pl.pallas_call(
        functools.partial(whole_kernel, zs, xs, ys),
        out_shape=(
            jax.ShapeDtypeStruct((1, 2, 2, lines, 2 * SIDE), F32),
            jax.ShapeDtypeStruct(probe.shape, F32),
        ),
        in_specs=[pl.BlockSpec(memory_space=pltpu.HBM)] * len(operands),
        out_specs=(pl.BlockSpec(memory_space=pltpu.VMEM),) * 2,
        scratch_shapes=[
            pltpu.SMEM(tile_of.shape, jnp.int32),
            pltpu.SMEM(offsets.shape, jnp.int32),
            pltpu.SMEM(owner_map.shape, jnp.int32),
            vmem(*tile.shape),
            vmem(*probe.shape),
            pltpu.VMEM(hi.shape, BF16),
            pltpu.VMEM(lo.shape, BF16),
            pltpu.VMEM(shuffle.shape, BF16),
            pltpu.VMEM((tiles, 1, HALF), jnp.int32),
            pltpu.VMEM((32, HALF), jnp.int32),
            pltpu.SMEM((32, HALF), jnp.int32),
            vmem(tiles * reads, piece, SIDE),
            vmem(tiles, MAX_READS, piece, SIDE),
            vmem(2, 8 * 2 * SIDE, HALF),
            vmem(MAX_READS, SIDE, SIDE),
            vmem(MAX_READS, 2, SIDE, SIDE),
            vmem(MAX_READS, 2, SIDE, SIDE),
            vmem(2, SIDE, HALF),
            vmem(2, 8 * 3 * SIDE, HALF),
            vmem(2, 8 * 2 * SIDE, HALF),
            vmem(2, SIDE, SIDE),
            vmem(4, 2, height, HALF),
            vmem(4, 2, height, HALF),
            vmem(2, height, HALF),
            vmem(4, height, HALF),
            vmem(SIDE, SIDE),
            vmem(tiles, piece, SIDE),
            vmem(4, piece, SIDE),
            dma((3,)), dma((5,)), dma, dma, dma((tiles,)), dma((tiles,)), dma((tiles,)), dma((tiles,)),
            dma((MAX_READS, tiles)), dma((MAX_READS, tiles)), dma((5,)), dma((5,)), dma((4,)), dma((4,)),
            dma((2, 2)), dma((2, 2)), dma((tiles,)), dma((tiles,)), dma((4,)), dma((4,)),
            dma((tiles,)), dma((tiles,)), dma, dma,
        ],
        cost_estimate=pl.CostEstimate(
            flops=MAX_READS * 50 * 2 * SIDE**3, bytes_accessed=10 << 20, transcendentals=0
        ),
        compiler_params=pltpu.CompilerParams(
            collective_id=0, has_side_effects=True, vmem_limit_bytes=56 << 20
        ),
    )(*(pltpu.with_memory_space_constraint(x, pltpu.HBM) for x in operands))


def per_device(object_tiles, probe_wave, patterns, tile_of, offsets, owner_map):
    tile_count = lax.axis_size("tile")
    high, low, shuffle = (jnp.asarray(table) for table in tables())
    zs, xs = lax.axis_size("scan") // CORES, math.isqrt(tile_count)
    ys = tile_count // xs
    object_part, probe_total = whole(
        zs, xs, ys,
        tile_of, offsets.T, owner_map, patterns, object_tiles, probe_wave, high, low, shuffle,
    )
    count = tile_count * lax.axis_size("scan") * patterns.shape[0]
    return object_part, probe_total / jnp.sqrt(jnp.ones((), F32) * count)


def solution(mesh):
    return jax.shard_map(
        per_device,
        mesh=mesh,
        in_specs=(
            P("tile", None, None, None, None),
            P(),
            P(("scan", "tile"), None, None),
            P(("scan", "tile")),
            P(("scan", "tile"), None),
            P(),
        ),
        out_specs=(P("tile", None, None, "scan", None), P()),
        check_vma=False,
    )
```

time: 88.9 us -> 85.9 us (0.966)
  Pallas kernels: 86.4 us -> 81.1 us
  local copies, waits for them, and re-layouts: 0.82 us -> 1.87 us
  other arithmetic: 0.84 us -> 1.88 us
    pallas_call x3 -> x1, Pallas kernels: 86.4 us -> 81.1 us  [whole(): pl.pallas_call(functools.partial(whole_kernel, zs, xs, ys), out_shape=(ja...]
    unnamed x9 -> x1, local copies, waits for them, and re-layouts: 0.82 us -> 1.87 us
    div x1, other arithmetic: 0.84 us -> 1.88 us  [per_device(): return (object_part, probe_total / jnp.sqrt(jnp.ones((), F32) * count))]
where the time goes in v7:
time: 85.9 us; the launch traced here: 85.5 us
  Pallas kernels  81.1 us (94%)
  other arithmetic  1.88 us (2%)
  local copies, waits for them, and re-layouts  1.87 us (2%)
    pallas_call x1, Pallas kernels, whole(): pl.pallas_call(functools.partial(whole_kernel, zs, xs, ys), out_shape=(ja...  81.1 us
    div x1, other arithmetic, per_device(): return (object_part, probe_total / jnp.sqrt(jnp.ones((), F32) * count))  1.88 us
    unnamed x1, local copies, waits for them, and re-layouts  1.87 us

profile of v7, /device:TPU:1, one launch (start us, length us, event | category | flops | bytes accessed | tf_op | source)
XLA Modules:
  0.0 85.5 jit_solution(4582996500109738223)
XLA Ops:
  0.6 81.1 %shard_map.104 = (f32[1,2,2,64,512]{4,3,2,1,0:T(8,128)}, f32[2,256,256]{2,1,0:T(8,128)}) custom-call(s32[4]{0:T(128)} %tile_hbm.1, s32[2,4]{1,0:T(2,128)} %bitcast.1, s32[16]{0:T(128)} %owner_hbm.1, f32[4,256,256]{2,1,0:T(8,128)} %patterns.1, f32[1,2,2,512,512]{4,3,2,1,0:T(8,128)} %tile.1, f32[2,256,256]{2,1,0:T(8,128)} %probe_hbm.1, ...), custom_call_target="tpu_custom_call" | custom-call | flops 13421772800 | bytes 10485760 | tf_op jit(solution)/shard_map/pallas_call | solution.py:506
  81.8 1.9 %broadcast_multiply_fusion = f32[2,256,256]{2,1,0:T(8,128)} fusion(f32[2,256,256]{2,1,0:T(8,128)} %get-tuple-element.5), kind=kLoop, calls=%fused_computation | loop fusion | flops 131072 | bytes 1048576 | tf_op jit(solution)/shard_map/div | solution.py:567
  83.7 1.9 %copy.12 = f32[1,2,2,64,512]{4,3,2,1,0:T(8,128)} copy(f32[1,2,2,64,512]{4,3,2,1,0:T(8,128)} %get-tuple-element.8) | data formatting | bytes 1048576

commit v8 on v7

--- a/solution.py
+++ b/solution.py
@@ -327,6 +327,11 @@
     ]
     for copy in tells + firsts:
         copy.start()
+    probe_grad[...] = jnp.zeros_like(probe_grad)
+    grad[...] = jnp.zeros_like(grad)
+    border = jnp.zeros((2, 8 * SIDE, HALF), F32)
+    padded[:, : 8 * SIDE, :] = border
+    padded[:, 16 * SIDE :, :] = border
     loads[0].wait()
     open_tile(opened.at[0], held)
     for copy in tells:
@@ -368,9 +373,6 @@
 
     lax.fori_loop(0, MAX_READS, send_rank, 0)
     lax.fori_loop(AHEAD, MAX_READS, run_forward, 0)
-    probe_grad[...] = jnp.zeros_like(probe_grad)
-    grad[...] = jnp.zeros_like(grad)
-    padded[...] = jnp.zeros_like(padded)
 
     def run_backward(k, carry):
         a, b = where(k)
@@ -385,7 +387,7 @@
                 place(padded.at[part], comp, b, values[comp])
         probe_grad[0] += probe_term[0]
         probe_grad[1] += probe_term[1]
-        lines = 256
+        lines = 512
 
         def add(i, inner):
             for part in range(2):
@@ -549,7 +551,7 @@
             flops=MAX_READS * 50 * 2 * SIDE**3, bytes_accessed=10 << 20, transcendentals=0
         ),
         compiler_params=pltpu.CompilerParams(
-            collective_id=0, has_side_effects=True, vmem_limit_bytes=56 << 20
+            collective_id=0, has_side_effects=True, vmem_limit_bytes=46 << 20
         ),
     )(*(pltpu.with_memory_space_constraint(x, pltpu.HBM) for x in operands))
 

time: 85.9 us -> 82.4 us (0.959)
  Pallas kernels: 81.1 us -> 80 us
  local copies, waits for them, and re-layouts: 1.87 us -> 0.79 us
  other arithmetic: 1.88 us -> 0.84 us
    pallas_call x1, Pallas kernels: 81.1 us -> 80 us  [whole(): pl.pallas_call(functools.partial(whole_kernel, zs, xs, ys), out_shape=(ja...]
    unnamed x1, local copies, waits for them, and re-layouts: 1.87 us -> 0.79 us
    div x1, other arithmetic: 1.88 us -> 0.84 us  [per_device(): return (object_part, probe_total / jnp.sqrt(jnp.ones((), F32) * count))]
where the time goes in v8:
time: 82.4 us; the launch traced here: 82.2 us
  Pallas kernels  80 us (97%)
  other arithmetic  0.84 us (1%)
    pallas_call x1, Pallas kernels, whole(): pl.pallas_call(functools.partial(whole_kernel, zs, xs, ys), out_shape=(ja...  80 us

profile of v8, /device:TPU:1, one launch (start us, length us, event | category | flops | bytes accessed | tf_op | source)
XLA Modules:
  0.0 82.2 jit_solution(463700944277744702)
XLA Ops:
  0.6 80.0 %shard_map.104 = (f32[1,2,2,64,512]{4,3,2,1,0:T(8,128)S(1)}, f32[2,256,256]{2,1,0:T(8,128)S(1)}) custom-call(s32[4]{0:T(128)} %tile_hbm.1, s32[2,4]{1,0:T(2,128)} %bitcast.1, s32[16]{0:T(128)} %owner_hbm.1, f32[4,256,256]{2,1,0:T(8,128)} %patterns.1, f32[1,2,2,512,512]{4,3,2,1,0:T(8,128)} %tile.1, f32[2,256,256]{2,1,0:T(8,128)} %probe_hbm.1, ...), custom_call_target="tpu_custom_call" | custom-call | flops 13421772800 | bytes 10485760 | tf_op jit(solution)/shard_map/pallas_call | solution.py:508
  80.6 0.8 %broadcast_multiply_fusion = f32[2,256,256]{2,1,0:T(8,128)} fusion(f32[2,256,256]{2,1,0:T(8,128)S(1)} %get-tuple-element.5), kind=kLoop, calls=%fused_computation | loop fusion | flops 131072 | bytes 1048576 | tf_op jit(solution)/shard_map/div | solution.py:569
  81.5 0.8 copy.12

commit v9 on v8

--- a/solution.py
+++ b/solution.py
@@ -188,7 +188,7 @@
     return back, to_far(re * ore - im * oim, re * oim + im * ore, hi, lo)
 
 
-def backward_one(k, a, b, valid, held, probe, hi, lo, shuffle, back, far, arrived, mixed):
+def backward_far(k, valid, hi, lo, shuffle, back, far, arrived, mixed):
     for c in range(2):
         mixed[c] = arrived[k, :, c * HALF : (c + 1) * HALF]
     measured = jnp.concatenate(
@@ -204,13 +204,16 @@
     scale = valid * (fre * fre + fim * fim - measured)
     gre, gim = from_far(scale * fre, scale * fim, hi, lo)
     bre, bim = back[k, 0], back[k, 1]
-    second = (bre * gre + bim * gim, bre * gim - bim * gre)
+    return (gre, gim), (bre * gre + bim * gim, bre * gim - bim * gre)
+
+
+def backward_near(a, b, gre, gim, held, probe, hi, lo):
     ore, oim = patch(held.at[1], 0, a, b), patch(held.at[1], 1, a, b)
     gre, gim = travel(ore * gre + oim * gim, ore * gim - oim * gre, hi, lo, True)
     pre, pim = probe[0], probe[1]
     first = (pre * gre + pim * gim, pre * gim - pim * gre)
     ore, oim = patch(held.at[0], 0, a, b), patch(held.at[0], 1, a, b)
-    return second, first, (ore * gre + oim * gim, ore * gim - oim * gre)
+    return first, (ore * gre + oim * gim, ore * gim - oim * gre)
 
 
 MESH = pl.DeviceIdType.MESH
@@ -268,7 +271,7 @@
     held, arrived, back, far, mixed, padded, grad, probe_grad,
     own, core_in, half_in, direct_in, plane_in, piece_in, piece_z,
     small_sem, load_sem, own_sem, list_sem, note_send, note_recv, first_send, first_recv,
-    second_send, second_recv, core_send, core_recv, ring_send, ring_recv, part_send, part_recv,
+    second_send, second_recv, core_send, core_recv, ring_send, ring_recv,
     probe_send, probe_recv, z_send, z_recv, all_send, all_recv, pair_send, pair_recv,
 ):
     scan = lax.axis_index("scan")
@@ -374,32 +377,41 @@
     lax.fori_loop(0, MAX_READS, send_rank, 0)
     lax.fori_loop(AHEAD, MAX_READS, run_forward, 0)
 
-    def run_backward(k, carry):
-        a, b = where(k)
+    def add_parts(a, b, values):
+        for part, pair_of in values.items():
+            for comp in range(2):
+                place(padded.at[part], comp, b, pair_of[comp])
+        lines = 512
+
+        def add(i, inner):
+            to = pl.ds(pl.multiple_of(i * lines, 8), lines)
+            source = pl.ds((SIDE - a + i * (lines // 8)) * 8, lines)
+            for part in values:
+                grad[part, to, :] = grad[part, to, :] + padded[part, source, :]
+            return inner
+
+        lax.fori_loop(0, 8 * 2 * SIDE // lines, add, 0)
+
+    def far_side(k):
         valid = jnp.where(k < lists_smem[24, me], 2.0, 0.0)
         for j in shifts:
             second(k, j).wait_recv()
-        slice1, slice0, probe_term = backward_one(
-            k, a, b, valid, held, probe, hi, lo, shuffle, back, far, arrived, mixed
-        )
-        for part, values in enumerate((slice0, slice1)):
-            for comp in range(2):
-                place(padded.at[part], comp, b, values[comp])
+        return backward_far(k, valid, hi, lo, shuffle, back, far, arrived, mixed)
+
+    def near_side(k, wave):
+        a, b = where(k)
+        slice0, probe_term = backward_near(a, b, *wave, held, probe, hi, lo)
         probe_grad[0] += probe_term[0]
         probe_grad[1] += probe_term[1]
-        lines = 512
-
-        def add(i, inner):
-            for part in range(2):
-                to = pl.ds(pl.multiple_of(i * lines, 8), lines)
-                source = pl.ds((SIDE - a + i * (lines // 8)) * 8, lines)
-                grad[part, to, :] = grad[part, to, :] + padded[part, source, :]
-            return inner
-
-        lax.fori_loop(0, 8 * 2 * SIDE // lines, add, 0)
+        return slice0
+
+    def run_backward(k, carry):
+        wave, slice1 = far_side(k)
+        slice0 = near_side(k, wave)
+        add_parts(*where(k), {0: slice0, 1: slice1})
         return carry
 
-    lax.fori_loop(0, MAX_READS, run_backward, 0)
+    lax.fori_loop(0, MAX_READS - 1, run_backward, 0)
 
     steps = [2, 1, -1, 0]
 
@@ -413,52 +425,71 @@
         started.append(copy)
         return copy
 
-    def core_copy(k):
-        return go(remote(grad.at[:, rows_of(steps[k], 1 - c), :], core_in.at[k], core_send.at[k], core_recv.at[k], pair))
-
-    cores = [core_copy(0)]
-    probe_pair = go(remote(probe_grad.at[1 - c], plane_in, core_send.at[4], core_recv.at[4], pair))
-    cores += [core_copy(k) for k in (1, 2, 3)]
-
-    def merge(k):
-        cores[k].wait_recv()
-        own[k] = grad[:, rows_of(steps[k], c), :] + core_in[k]
-
-    def direct(part):
-        half = pl.ds(part * (height // 2), height // 2)
+    up_rows, down_rows = pl.ds(0, height // 2), pl.ds(height // 2, height // 2)
+
+    def core_copy(k, p):
+        return go(remote(grad.at[p, rows_of(steps[k], 1 - c), :], core_in.at[k, p], core_send.at[k, p], core_recv.at[k, p], pair))
+
+    def merge(copy, k, p):
+        copy.wait_recv()
+        own[k, p] = grad[p, rows_of(steps[k], c), :] + core_in[k, p]
+
+    def hop(src, dst, kind, p, way):
+        return go(remote(src, dst, ring_send.at[kind, p, way], ring_recv.at[kind, p, way], at_z(1 - 2 * way)))
+
+    def farthest(p):
         return [
-            go(remote(own.at[1, 1, half], direct_in.at[0, half], part_send.at[0, part], part_recv.at[0, part], at_z(1))),
-            go(remote(own.at[2, 0, half], direct_in.at[1, half], part_send.at[1, part], part_recv.at[1, part], at_z(-1))),
+            hop(own.at[0, p, up_rows], half_in.at[p, 0], 0, p, 0),
+            hop(own.at[0, p, down_rows], half_in.at[p, 1], 0, p, 1),
         ]
 
-    merge(0)
-    halves = [
-        go(remote(own.at[0, 0], half_in.at[0], ring_send.at[0], ring_recv.at[0], at_z(1))),
-        go(remote(own.at[0, 1], half_in.at[1], ring_send.at[1], ring_recv.at[1], at_z(-1))),
-    ]
+    def straight(p):
+        return [
+            hop(own.at[1, p, down_rows], direct_in.at[p, 0], 1, p, 0),
+            hop(own.at[2, p, up_rows], direct_in.at[p, 1], 1, p, 1),
+        ]
+
+    def summed(p, halves):
+        halves[0].wait_recv()
+        own[1, p, up_rows] = own[1, p, up_rows] + half_in[p, 0]
+        first = hop(own.at[1, p, up_rows], direct_in.at[p, 2], 2, p, 0)
+        halves[1].wait_recv()
+        own[2, p, down_rows] = own[2, p, down_rows] + half_in[p, 1]
+        return [first, hop(own.at[2, p, down_rows], direct_in.at[p, 3], 2, p, 1)]
+
+    final = MAX_READS - 1
+    wave, slice1 = far_side(final)
+    add_parts(*where(final), {1: slice1})
+    cores1 = [core_copy(k, 1) for k in range(4)]
+    slice0 = near_side(final, wave)
+    probe_pair = go(remote(probe_grad.at[1 - c], plane_in, pair_send.at[0], pair_recv.at[0], pair))
+    for k in range(3):
+        merge(cores1[k], k, 1)
+        if k == 0:
+            halves1 = farthest(1)
+    waits = straight(1)
     probe_pair.wait_recv()
     plane_in[...] = plane_in[...] + probe_grad[c]
     gathers = [
         go(remote(plane_in.at[piece_rows(at_xy(j)["tile"])], piece_in.at[j], probe_send.at[j], probe_recv.at[j], at_xy(j)))
         for j in shifts
     ]
-    merge(1)
-    merge(2)
-    straight = direct(0)
-    merge(3)
+    add_parts(*where(final), {0: slice0})
+    cores0 = [core_copy(k, 0) for k in range(4)]
+    merge(cores0[0], 0, 0)
+    halves0 = farthest(0)
+    for k in range(1, 4):
+        merge(cores0[k], k, 0)
+    merge(cores1[3], 3, 1)
     total = plane_in[piece_rows(me), :]
     for copy, j in zip(gathers, shifts):
         copy.wait_recv()
         total = total + piece_in[j]
     piece_z[0] = total
     across = [go(remote(piece_z.at[0], piece_z.at[k], z_send.at[k], z_recv.at[k], at_z(k))) for k in (1, 2, 3)]
-    straight += direct(1)
-    halves[0].wait_recv()
-    own[1, 0] = own[1, 0] + half_in[0]
-    up_sum = go(remote(own.at[1, 0], direct_in.at[2], ring_send.at[2], ring_recv.at[2], at_z(1)))
-    halves[1].wait_recv()
-    own[2, 1] = own[2, 1] + half_in[1]
-    down_sum = go(remote(own.at[2, 1], direct_in.at[3], ring_send.at[3], ring_recv.at[3], at_z(-1)))
+    waits += summed(1, halves1)
+    waits += straight(0)
+    waits += summed(0, halves0)
     for copy in across:
         copy.wait_recv()
     probe_out[c, piece_rows(me), :] = (piece_z[0] + piece_z[1]) + (piece_z[2] + piece_z[3])
@@ -468,13 +499,12 @@
     ]
     for copy in spreads:
         copy.wait_recv()
-    last = go(remote(probe_out.at[c], probe_out.at[c], pair_send, pair_recv, pair))
-    for copy in straight:
+    last = go(remote(probe_out.at[c], probe_out.at[c], pair_send.at[1], pair_recv.at[1], pair))
+    for copy in waits:
         copy.wait_recv()
-    up_sum.wait_recv()
-    down_sum.wait_recv()
-    own[3, 0] = own[3, 0] + (direct_in[2] + direct_in[1])
-    own[3, 1] = own[3, 1] + (direct_in[0] + direct_in[3])
+    for p in range(2):
+        own[3, p, up_rows] = own[3, p, up_rows] + (direct_in[p, 2] + direct_in[p, 1])
+        own[3, p, down_rows] = own[3, p, down_rows] + (direct_in[p, 0] + direct_in[p, 3])
     lines = out.shape[3]
     for plane in range(4):
         for k in range(4):
@@ -537,15 +567,15 @@
             vmem(2, SIDE, SIDE),
             vmem(4, 2, height, HALF),
             vmem(4, 2, height, HALF),
-            vmem(2, height, HALF),
-            vmem(4, height, HALF),
+            vmem(2, 2, height // 2, HALF),
+            vmem(2, 4, height // 2, HALF),
             vmem(SIDE, SIDE),
             vmem(tiles, piece, SIDE),
             vmem(4, piece, SIDE),
             dma((3,)), dma((5,)), dma, dma, dma((tiles,)), dma((tiles,)), dma((tiles,)), dma((tiles,)),
-            dma((MAX_READS, tiles)), dma((MAX_READS, tiles)), dma((5,)), dma((5,)), dma((4,)), dma((4,)),
-            dma((2, 2)), dma((2, 2)), dma((tiles,)), dma((tiles,)), dma((4,)), dma((4,)),
-            dma((tiles,)), dma((tiles,)), dma, dma,
+            dma((MAX_READS, tiles)), dma((MAX_READS, tiles)), dma((4, 2)), dma((4, 2)),
+            dma((3, 2, 2)), dma((3, 2, 2)), dma((tiles,)), dma((tiles,)), dma((4,)), dma((4,)),
+            dma((tiles,)), dma((tiles,)), dma((2,)), dma((2,)),
         ],
         cost_estimate=pl.CostEstimate(
             flops=MAX_READS * 50 * 2 * SIDE**3, bytes_accessed=10 << 20, transcendentals=0
@@ -556,6 +586,22 @@
     )(*(pltpu.with_memory_space_constraint(x, pltpu.HBM) for x in operands))
 
 
+def close_kernel(scale, object_in, probe_in, object_out, probe_out):
+    object_out[...] = object_in[...]
+    probe_out[...] = probe_in[...] * scale
+
+
+def close(scale, object_part, probe_total):
+    vmem = pl.BlockSpec(memory_space=pltpu.VMEM)
+    return pl.pallas_call(
+        functools.partial(close_kernel, scale),
+        out_shape=tuple(jax.ShapeDtypeStruct(x.shape, F32) for x in (object_part, probe_total)),
+        in_specs=[vmem, vmem],
+        out_specs=(vmem, vmem),
+        compiler_params=pltpu.CompilerParams(vmem_limit_bytes=4 << 20),
+    )(object_part, probe_total)
+
+
 def per_device(object_tiles, probe_wave, patterns, tile_of, offsets, owner_map):
     tile_count = lax.axis_size("tile")
     high, low, shuffle = (jnp.asarray(table) for table in tables())
@@ -566,7 +612,7 @@
         tile_of, offsets.T, owner_map, patterns, object_tiles, probe_wave, high, low, shuffle,
     )
     count = tile_count * lax.axis_size("scan") * patterns.shape[0]
-    return object_part, probe_total / jnp.sqrt(jnp.ones((), F32) * count)
+    return close(1.0 / math.sqrt(count), object_part, probe_total)
 
 
 def solution(mesh):

time: 82.4 us -> 81.5 us (0.989)
  other arithmetic: 0.84 us -> 0 us
    pallas_call x0 -> x1, Pallas kernels: none -> 1.05 us  [close(): pl.pallas_call(functools.partial(close_kernel, scale), out_shape=tuple((j...]
    div x1 -> x0, other arithmetic: 0.84 us -> none  [per_device(): return (object_part, probe_total / jnp.sqrt(jnp.ones((), F32) * count))]
where the time goes in v9:
time: 81.5 us; the launch traced here: 81.4 us
  Pallas kernels  80.8 us (99%)
    pallas_call x1, Pallas kernels, whole(): pl.pallas_call(functools.partial(whole_kernel, zs, xs, ys), out_shape=(ja...  79.7 us

profile of v9, /device:TPU:1, one launch (start us, length us, event | category | flops | bytes accessed | tf_op | source)
XLA Modules:
  0.0 81.4 jit_solution(10792998111958292761)
XLA Ops:
  0.6 79.7 %shard_map.104 = (f32[1,2,2,64,512]{4,3,2,1,0:T(8,128)S(1)}, f32[2,256,256]{2,1,0:T(8,128)S(1)}) custom-call(s32[4]{0:T(128)} %tile_hbm.1, s32[2,4]{1,0:T(2,128)} %bitcast.1, s32[16]{0:T(128)} %owner_hbm.1, f32[4,256,256]{2,1,0:T(8,128)} %patterns.1, f32[1,2,2,512,512]{4,3,2,1,0:T(8,128)} %tile.1, f32[2,256,256]{2,1,0:T(8,128)} %probe_hbm.1, ...), custom_call_target="tpu_custom_call" | custom-call | flops 13421772800 | bytes 10485760 | tf_op jit(solution)/shard_map/pallas_call | solution.py:538
  80.4 1.0 %shard_map.105 = (f32[1,2,2,64,512]{4,3,2,1,0:T(8,128)}, f32[2,256,256]{2,1,0:T(8,128)}) custom-call(f32[1,2,2,64,512]{4,3,2,1,0:T(8,128)S(1)} %get-tuple-element.4.object_in, f32[2,256,256]{2,1,0:T(8,128)S(1)} %get-tuple-element.5.probe_in), custom_call_target="tpu_custom_call" | custom-call | tf_op jit(solution)/shard_map/pallas_call | solution.py:596

commit v10 on v9

--- a/solution.py
+++ b/solution.py
@@ -234,7 +234,11 @@
     def at_xy(j):
         return {"tile": lax.rem(x + j // ys, xs) * ys + lax.rem(y + j % ys, ys)}
 
-    return tile, at_xy, range(1, xs * ys)
+    def hops(j):
+        dx, dy = j // ys, j % ys
+        return min(dx, xs - dx) + min(dy, ys - dy)
+
+    return tile, at_xy, sorted(range(1, xs * ys), key=lambda j: -hops(j))
 
 
 def read_lists(notes, tables_ref):

time: 81.5 us -> 85.2 us (1.045)
  Pallas kernels: 80.8 us -> 84.2 us
    pallas_call x1, Pallas kernels: 79.7 us -> 83.1 us  [whole(): pl.pallas_call(functools.partial(whole_kernel, zs, xs, ys), out_shape=(ja...]
where the time goes in v10:
time: 85.2 us; the launch traced here: 84.8 us
  Pallas kernels  84.2 us (99%)
    pallas_call x1, Pallas kernels, whole(): pl.pallas_call(functools.partial(whole_kernel, zs, xs, ys), out_shape=(ja...  83.1 us

profile of v10, /device:TPU:1, one launch (start us, length us, event | category | flops | bytes accessed | tf_op | source)
XLA Modules:
  0.0 84.8 jit_solution(14655667500272658620)
XLA Ops:
  0.6 83.1 %shard_map.104 = (f32[1,2,2,64,512]{4,3,2,1,0:T(8,128)S(1)}, f32[2,256,256]{2,1,0:T(8,128)S(1)}) custom-call(s32[4]{0:T(128)} %tile_hbm.1, s32[2,4]{1,0:T(2,128)} %bitcast.1, s32[16]{0:T(128)} %owner_hbm.1, f32[4,256,256]{2,1,0:T(8,128)} %patterns.1, f32[1,2,2,512,512]{4,3,2,1,0:T(8,128)} %tile.1, f32[2,256,256]{2,1,0:T(8,128)} %probe_hbm.1, ...), custom_call_target="tpu_custom_call" | custom-call | flops 13421772800 | bytes 10485760 | tf_op jit(solution)/shard_map/pallas_call | solution.py:542
  83.8 1.0 %shard_map.105 = (f32[1,2,2,64,512]{4,3,2,1,0:T(8,128)}, f32[2,256,256]{2,1,0:T(8,128)}) custom-call(f32[1,2,2,64,512]{4,3,2,1,0:T(8,128)S(1)} %get-tuple-element.4.object_in, f32[2,256,256]{2,1,0:T(8,128)S(1)} %get-tuple-element.5.probe_in), custom_call_target="tpu_custom_call" | custom-call | tf_op jit(solution)/shard_map/pallas_call | solution.py:600
